TPU v7x, 128 devices: a whole 4x4x4 slice. The times are simulated.
128 devices in a mesh: tok: 16 (over x, z), head: 8 (over y, core).
Axes of the slice: x: 4, y: 4, z: 4, core: 2. Of those that a mesh axis runs over, the one named last changes fastest.
Arguments:
- tokens: bfloat16 [4096, 2880], P(('tok', 'head')), may hold values from -6 to 6
- lengths: int32 [4], replicated, may hold values from 1 to 2048, 3968 in all
- norm_gain_attn: float32 [2880], replicated, may hold values from 0.1 to 1.9
- query_key_value_weight: bfloat16 [2880, 5120], P(None, 'head'), may hold values from -0.109375 to 0.109375
- sinks: float32 [64], P('head'), may hold values from 1 to 6
- w_out_attn: bfloat16 [4096, 2880], P('head'), may hold values from -0.09375 to 0.09375
- norm_gain_moe: float32 [2880], replicated, may hold values from 0.1 to 1.9
- routes: int32 [4096, 4], P(('tok', 'head')), may hold values from 0 to 31, all different within a row; in each aligned block of 32 rows (0 to 31, 32 to 63, ...) at most 6 rows name the same one
- gates: float32 [4096, 4], P(('tok', 'head')), may hold values from 0.1 to 1
- w_in: bfloat16 [128, 2880, 1440], P(('tok', 'head')), may hold values from -0.109375 to 0.109375
- w_down: bfloat16 [128, 720, 2880], P(('tok', 'head')), may hold values from -0.109375 to 0.109375
- page_table: int32 [256], replicated, may hold values from 0 to 255, as said below
Outputs:
- hidden_out: bfloat16 [4096, 2880], P(('tok', 'head'))
- kv_cache: bfloat16 [8, 256, 16, 128], P('head', 'tok')
Inputs may be any that keep to these rules, and one draw needn't show every extreme that they name: `routes`: every row names 4 different experts. In each aligned block of 32 rows no expert is named by more than 6 rows, and in every draw some block has an expert named by exactly 6 rows. `lengths`: they sum to 3968, and the longest is exactly 2048. `page_table`: A permutation. Of the 16 logical pages in each aligned block of 16, exactly 1 map into each aligned block of 16 physical pages.
All inputs are finite; a program needn't handle non-finite values.
Results may differ from a plain program's by a relative error of at most 0.018.
Values may be sent and summed in bfloat16 or wider, within the bound.
A program may use at most 128 MiB of HBM per device.

v0:
```python
import math

import jax
import jax.numpy as jnp
from jax import lax
from jax.sharding import PartitionSpec as P

MODEL_WIDTH = 2880
HEAD_SIZE = 64
EXPERTS = 32
ATTEND_WINDOW = 128
NSEQ = 4
PAGE_TOKENS = 16
QUERY_PER_KEY = 8


EPSILON = 1e-05
ROPE_BASE = 150000.0
GLU_ALPHA = 1.702


def passed_along(array, axis, by):
    peers = lax.axis_size(axis)
    pairs = [(i, i + by) for i in range(peers) if 0 <= i + by < peers]
    return lax.ppermute(array, axis, pairs)


def normalize(values, gain_vec):
    wide = values.astype(jnp.float32)
    inv_rms = lax.rsqrt(jnp.mean(wide * wide, axis=-1, keepdims=True) + EPSILON)
    return wide * inv_rms * gain_vec


def segment_table(lengths, row_index):
    seq_ends = jnp.cumsum(lengths)
    starts = jnp.concatenate([jnp.zeros((1,), jnp.int32), seq_ends])
    segment = jnp.sum((row_index[:, None] >= seq_ends[None, :]).astype(jnp.int32), axis=1)
    onehot = segment[:, None] == jnp.arange(starts.shape[0], dtype=jnp.int32)[None, :]
    seg_start = jnp.sum(jnp.where(onehot, starts[None, :], 0), axis=1)
    return (segment, row_index - seg_start)


def rotate(values, positions):
    half_dim = values.shape[-1] // 2
    inv_freq = jnp.exp(
        jnp.arange(half_dim, dtype=jnp.float32) * (-2.0 * math.log(ROPE_BASE) / values.shape[-1])
    )
    angles = positions.astype(jnp.float32)[:, None] * inv_freq[None, :]
    view_shape = (angles.shape[0],) + (1,) * (values.ndim - 2) + (half_dim,)
    cos_table = jnp.cos(angles).reshape(view_shape)
    sin_table = jnp.sin(angles).reshape(view_shape)
    lower_half = values[..., :half_dim]
    upper_half = values[..., half_dim:]
    return jnp.concatenate(
        [
            lower_half * cos_table - upper_half * sin_table,
            upper_half * cos_table + lower_half * sin_table,
        ],
        axis=-1,
    )


def band_mask(query_index, key_index, query_segs, key_segs, window):
    nblocks = query_index.shape[0] // window
    query_pos = query_index.reshape(nblocks, window)
    query_seg = query_segs.reshape(nblocks, window)
    key_grid = key_index.reshape(nblocks + 1, window)
    seg_grid = key_segs.reshape(nblocks + 1, window)
    key_pos = jnp.concatenate([key_grid[:-1], key_grid[1:]], axis=1)
    key_seg = jnp.concatenate([seg_grid[:-1], seg_grid[1:]], axis=1)
    distance = query_pos[:, :, None] - key_pos[:, None, :]
    allowed = (query_seg[:, :, None] == key_seg[:, None, :]) & (query_seg < NSEQ)[:, :, None]
    allowed = allowed & (key_pos >= 0)[:, None, :] & (distance >= 0) & (distance < window)
    return allowed


def band_attention(query_rows, extended, sink_table, allowed):
    nblocks = allowed.shape[0]
    groups = sink_table.shape[0]
    query_blocks = query_rows.reshape(nblocks, ATTEND_WINDOW, groups, QUERY_PER_KEY, HEAD_SIZE)
    pair_grid = extended.reshape(nblocks + 1, ATTEND_WINDOW, groups, 2 * HEAD_SIZE)
    key_band = jnp.concatenate([pair_grid[:-1], pair_grid[1:]], axis=1)
    scores = jnp.einsum(
        "bqgnh,bkgh->bgnqk",
        query_blocks,
        key_band[..., :HEAD_SIZE],
        preferred_element_type=jnp.float32,
    )
    weights = jnp.where(allowed[:, None, None], jnp.exp(scores), 0.0)
    totals = jnp.sum(weights, axis=-1, keepdims=True) + jnp.exp(sink_table)[None, :, :, None, None]
    probs_bf = (weights / totals).astype(jnp.bfloat16)
    outputs = jnp.einsum(
        "bgnqk,bkgh->bqgnh", probs_bf, key_band[..., HEAD_SIZE:], preferred_element_type=jnp.float32
    )
    return outputs.astype(jnp.bfloat16).reshape(
        nblocks * ATTEND_WINDOW, groups * QUERY_PER_KEY * HEAD_SIZE
    )


def expert_mlp(rows_in, w_in_local, w_down_local):
    ffs_local = w_down_local.shape[0]
    gate_up = jnp.dot(rows_in, w_in_local, preferred_element_type=jnp.float32)
    gate_part = gate_up[:, :ffs_local]
    up_part = gate_up[:, ffs_local:]
    activated = ((up_part + 1.0) * gate_part * jax.nn.sigmoid(GLU_ALPHA * gate_part)).astype(
        jnp.bfloat16
    )
    return jnp.dot(activated, w_down_local, preferred_element_type=jnp.float32).astype(jnp.bfloat16)


def copied_route(outgoing, route, width_split, slots, w_in_local, w_down_local):
    spread = jnp.broadcast_to(
        outgoing[:, None], (EXPERTS, width_split, slots, MODEL_WIDTH)
    ).reshape(EXPERTS * width_split, slots, MODEL_WIDTH)
    incoming = route(spread)
    produced = expert_mlp(incoming.reshape(-1, MODEL_WIDTH), w_in_local, w_down_local).reshape(
        spread.shape
    )
    returned = route(produced)
    return jnp.sum(
        returned.astype(jnp.float32).reshape(EXPERTS, width_split, slots, MODEL_WIDTH), axis=1
    ).reshape(EXPERTS * slots, MODEL_WIDTH)


def page_order(page_table, n_tok, pages_dev):
    page_grid = page_table.reshape(n_tok, pages_dev)
    target = page_grid // pages_dev
    page_ids = jnp.arange(pages_dev, dtype=jnp.int32)
    earlier = page_ids[:, None] > page_ids[None, :]
    same_dest = target[:, :, None] == target[:, None, :]
    order_rank = jnp.sum((same_dest & earlier[None]).astype(jnp.int32), axis=2)
    return (target, order_rank, page_grid % pages_dev)


def per_device(
    tokens,
    lengths,
    norm_gain_attn,
    query_key_value_weight,
    sinks,
    w_out_attn,
    norm_gain_moe,
    routes,
    gates,
    w_in,
    w_down,
    page_table,
):
    n_tok = lax.axis_size("tok")
    n_head = lax.axis_size("head")
    tok_id = lax.axis_index("tok")
    head_id = lax.axis_index("head")
    row_count = tokens.shape[0]
    tok_dev = row_count * n_head
    groups = sinks.shape[0] // QUERY_PER_KEY
    normed_input = normalize(tokens, norm_gain_attn).astype(jnp.bfloat16)
    projected_rows = jnp.dot(
        lax.all_gather(normed_input, "head", axis=0, tiled=True),
        query_key_value_weight,
        preferred_element_type=jnp.float32,
    ).reshape(tok_dev, groups, QUERY_PER_KEY + 2, HEAD_SIZE)
    row_base = tok_id * tok_dev
    query_index = row_base + jnp.arange(tok_dev, dtype=jnp.int32)
    query_segs, positions = segment_table(lengths, query_index)
    query_rows = (
        rotate(projected_rows[:, :, :QUERY_PER_KEY], positions) * HEAD_SIZE ** (-0.5)
    ).astype(jnp.bfloat16)
    key_rot = rotate(projected_rows[:, :, QUERY_PER_KEY], positions)
    key_value_pairs = jnp.concatenate(
        [key_rot, projected_rows[:, :, QUERY_PER_KEY + 1]], axis=-1
    ).astype(jnp.bfloat16)
    rim_rows = passed_along(key_value_pairs[tok_dev - ATTEND_WINDOW :], "tok", 1)
    key_index = row_base - ATTEND_WINDOW + jnp.arange(tok_dev + ATTEND_WINDOW, dtype=jnp.int32)
    key_segs, _ = segment_table(lengths, key_index)
    allowed = band_mask(query_index, key_index, query_segs, key_segs, ATTEND_WINDOW)
    attended = band_attention(
        query_rows,
        jnp.concatenate([rim_rows, key_value_pairs], axis=0),
        sinks.reshape(groups, QUERY_PER_KEY),
        allowed,
    )
    attn_sum = lax.psum_scatter(
        jnp.dot(attended, w_out_attn, preferred_element_type=jnp.float32).astype(jnp.bfloat16),
        "head",
        scatter_dimension=0,
        tiled=True,
    ).astype(jnp.float32)
    resid = tokens.astype(jnp.float32) + attn_sum
    moe_in = normalize(resid, norm_gain_moe).astype(jnp.bfloat16)
    own_index = row_base + head_id * row_count + jnp.arange(row_count, dtype=jnp.int32)
    own_segs, _ = segment_table(lengths, own_index)
    is_live = own_segs < NSEQ
    capacity = row_count // 8 + 2
    width_split = n_tok * n_head // EXPERTS
    expert_ids = jnp.arange(EXPERTS, dtype=jnp.int32)
    naming = routes[:, :, None] == expert_ids[None, None, :]
    routed = (jnp.any(naming, axis=1) & is_live[:, None]).astype(jnp.int32)
    slot_rank = jnp.cumsum(routed, axis=0) - 1
    slot_ids = jnp.arange(capacity, dtype=jnp.int32)
    placed = (routed == 1)[:, :, None] & (slot_rank[:, :, None] == slot_ids[None, None, :])
    local_ids = jnp.arange(row_count, dtype=jnp.int32)
    source_row = jnp.sum(jnp.where(placed, local_ids[:, None, None], 0), axis=0)
    filled = jnp.any(placed, axis=0)
    outgoing = jnp.where(filled[:, :, None], moe_in[source_row], jnp.zeros((), jnp.bfloat16))

    def flat_route(blocks):
        return lax.all_to_all(blocks, ("tok", "head"), split_axis=0, concat_axis=0, tiled=True)

    summed = copied_route(outgoing, flat_route, width_split, capacity, w_in[0], w_down[0])
    chosen_rank = jnp.sum(jnp.where(naming, slot_rank[:, None, :], 0), axis=2)
    pick_rows = routes * capacity + jnp.clip(chosen_rank, 0, capacity - 1)
    weighted = jnp.where(is_live[:, None], gates, 0.0)
    expert_sum = jnp.sum(summed[pick_rows] * weighted[:, :, None], axis=1)
    hidden_out = (resid + expert_sum).astype(jnp.bfloat16)
    pages_dev = tok_dev // PAGE_TOKENS
    share_count = pages_dev // n_tok
    paged = key_value_pairs.reshape(pages_dev, PAGE_TOKENS, groups, 2 * HEAD_SIZE)
    target, order_rank, slot_grid = page_order(page_table, n_tok, pages_dev)
    dest_ids = jnp.arange(n_tok, dtype=jnp.int32)
    share_ids = jnp.arange(share_count, dtype=jnp.int32)
    page_ids = jnp.arange(pages_dev, dtype=jnp.int32)
    my_target = target[tok_id]
    my_rank = order_rank[tok_id]
    matched = (my_target[:, None, None] == dest_ids[None, :, None]) & (
        my_rank[:, None, None] == share_ids[None, None, :]
    )
    pick_page = jnp.sum(jnp.where(matched, page_ids[:, None, None], 0), axis=0)
    arrived = lax.all_to_all(paged[pick_page], "tok", split_axis=0, concat_axis=0, tiled=True)
    to_here = (target == tok_id)[:, :, None] & (order_rank[:, :, None] == share_ids[None, None, :])
    landing = jnp.sum(jnp.where(to_here, slot_grid[:, :, None], 0), axis=1)
    stored = jnp.zeros_like(paged).at[landing.reshape(-1)].set(arrived.reshape(paged.shape))
    kv_cache = jnp.transpose(stored, (2, 0, 1, 3))
    return (hidden_out, kv_cache)


def solution(mesh):
    return jax.shard_map(
        per_device,
        mesh=mesh,
        in_specs=(
            P(("tok", "head"), None),
            P(),
            P(),
            P(None, "head"),
            P("head"),
            P("head", None),
            P(),
            P(("tok", "head"), None),
            P(("tok", "head"), None),
            P(("tok", "head"), None, None),
            P(("tok", "head"), None, None),
            P(),
        ),
        out_specs=(P(("tok", "head"), None), P("head", "tok", None, None)),
        check_vma=False,
    )
```

profile of v0, /device:TPU:2, one launch (start us, length us, event | category | flops | bytes accessed | tf_op | source)
XLA Modules:
  0.0 337.0 jit_solution(5325949729311232361)
XLA Ops:
  7.2 1.2 fusion.13
  8.5 1.7 fusion.15
  10.3 1.2 exp.30
  11.5 0.8 reduce-window.8
  12.8 0.1 copy-done.12
  12.9 0.8 multiply_cosine_fusion
  13.7 0.9 fusion.22
  14.6 22.3 %all-gather.2.cloned.1.call-done = bf16[256,2880]{1,0:T(8,128)(2,1)} async-done(((bf16[32,2880]{1,0:T(8,128)(2,1)}), bf16[256,2880]{1,0:T(8,128)(2,1)}) %all-gather.2.cloned.1.call-update) | async-done | bytes 1474576 | tf_op jit(solution)/shard_map/all_gather | solution.py:158
  36.9 4.1 %fusion.49 = f32[256,640]{0,1:T(8,128)S(1)} fusion(bf16[256,2880]{1,0:T(8,128)(2,1)} %all-gather.2.cloned.1.call-done, bf16[2880,640]{1,0:T(8,128)(2,1)} %param.15), kind=kOutput, calls=%fused_computation.145 | convolution fusion | flops 943718400 | bytes 5816320 | tf_op jit(solution)/shard_map/dot_general | solution.py:157
  41.1 0.2 fusion.31
  41.3 0.6 pad_maximum_fusion.3
  41.9 3.5 %collective-permute-start = (bf16[128,1,128]{0,2,1:T(8,128)(2,1)}, bf16[128,1,128]{0,2,1:T(8,128)(2,1)}, u32[]{:S(2)}, u32[]{:S(2)}) collective-permute-start(bf16[128,1,128]{0,2,1:T(8,128)(2,1)} %pad_maximum_fusion.3), channel_id=1, source_target_pairs={{0,8},{8,16},{16,24},{24,32},{32,40},{40,48},{48,56},{56,64},{64,7... | collective-permute-start | bytes 98312 | tf_op jit(solution)/shard_map/ppermute | solution.py:25
  45.5 0.6 copy_bitcast_fusion
  46.1 0.6 slice.143
  46.7 1.4 concatenate.80
  48.1 1.4 copy.75
  49.4 0.8 concatenate.85
  50.2 1.7 copy.77
  51.9 0.1 concatenate.86
  52.1 0.8 pad_maximum_fusion
  52.9 0.1 copy.72
  53.0 0.1 copy.76
  53.2 0.8 maximum_maximum_fusion
  53.9 1.5 fusion.6
  55.5 0.5 fusion.7
  56.0 0.3 copy.80
  56.4 2.2 convolution_convert_fusion.1
  59.1 0.1 reshape.833
  59.2 0.1 copy.81
  59.4 32.2 %reduce-scatter.2.cloned.1.call-done = bf16[32,2880]{1,0:T(8,128)(2,1)} async-done(((bf16[256,2880]{1,0:T(8,128)(2,1)}), bf16[32,2880]{1,0:T(8,128)(2,1)}) %reduce-scatter.2.cloned.1.call-update) | async-done | bytes 184336 | tf_op jit(solution)/shard_map/reduce_scatter | solution.py:182
  91.5 1.1 multiply_reduce_fusion.1
  92.7 1.0 multiply_convert_fusion
  93.7 1.3 gather_fusion
  95.1 1.4 reshape.832
  96.4 1.6 broadcast_select_fusion
  98.0 3.0 broadcast_in_dim.93
  101.1 7.4 %all-to-all-start = ((bf16[128,6,2880]{2,1,0:T(8,128)(2,1)}), bf16[128,6,2880]{2,1,0:T(8,128)(2,1)}, u32[]{:S(2)}, u32[]{:S(2)}) async-start(bf16[128,6,2880]{2,1,0:T(8,128)(2,1)} %bitcast.119), calls=%async_computation.1 | async-start | bytes 12058624 | tf_op jit(solution)/shard_map/all_to_all | solution.py:207
  108.6 0.4 convert_reduce_fusion.1
  109.0 0.1 select_reduce_fusion.2
  109.2 0.1 copy.86
  109.3 0.1 copy.87
  109.4 0.1 copy.88
  109.5 0.1 maximum_bitcast_fusion
  109.6 1.2 gather_fusion.2
  110.8 70.6 %all-to-all-done = bf16[128,6,2880]{2,1,0:T(8,128)(2,1)} async-done(((bf16[128,6,2880]{2,1,0:T(8,128)(2,1)}), bf16[128,6,2880]{2,1,0:T(8,128)(2,1)}, u32[]{:S(2)}, u32[]{:S(2)}) %all-to-all-start) | async-done | bytes 4423712 | tf_op jit(solution)/shard_map/all_to_all | solution.py:207
  181.5 7.4 %all-to-all-start.2 = ((bf16[16,1,16,1,128]{4,2,3,1,0:T(8,128)(2,1)}), bf16[16,1,16,1,128]{4,2,3,1,0:T(8,128)(2,1)S(1)}, u32[]{:S(2)}, u32[]{:S(2)}) async-start(bf16[16,1,16,1,128]{4,2,3,1,0:T(8,128)(2,1)} %bitcast.37), calls=%async_computation.3 | async-start | bytes 131072 | tf_op jit(solution)/shard_map/all_to_all | solution.py:228
  188.9 8.2 %reshape.821 = bf16[768,2880]{1,0:T(8,128)(2,1)} reshape(bf16[128,6,2880]{2,1,0:T(8,128)(2,1)} %all-to-all-done) | data formatting | bytes 8847360 | tf_op jit(solution)/shard_map/reshape | solution.py:116
  197.1 10.8 %fusion = f32[768,1440]{0,1:T(8,128)S(1)} fusion(bf16[768,2880]{1,0:T(8,128)(2,1)} %reshape.821, bf16[1,2880,1440]{1,2,0:T(8,128)(2,1)} %param.21), kind=kOutput, calls=%fused_computation.5 | convolution fusion | flops 6370099200 | bytes 17141760 | tf_op jit(solution)/shard_map/dot_general | solution.py:102
  207.9 8.1 %convolution_convert_fusion = bf16[768,2880]{0,1:T(8,128)(2,1)} fusion(bf16[1,720,2880]{2,1,0:T(8,128)(2,1)} %param.22, f32[768,1440]{0,1:T(8,128)S(1)} %fusion), kind=kOutput, calls=%fused_computation.7 | convolution fusion | flops 3191685120 | bytes 12994560 | tf_op jit(solution)/shard_map/dot_general | solution.py:108
  216.0 6.5 %copy.83 = bf16[768,2880]{1,0:T(8,128)(2,1)} copy(bf16[768,2880]{0,1:T(8,128)(2,1)} %convolution_convert_fusion) | data formatting | bytes 8847360 | tf_op jit(solution)/shard_map/convert_element_type | solution.py:108
  222.5 7.6 %reshape.822 = bf16[128,6,2880]{2,1,0:T(8,128)(2,1)} reshape(bf16[768,2880]{1,0:T(8,128)(2,1)} %copy.83) | data formatting | bytes 8847360 | tf_op jit(solution)/shard_map/reshape | solution.py:116
  230.1 7.4 %all-to-all-start.1 = ((bf16[128,6,2880]{2,1,0:T(8,128)(2,1)}), bf16[128,6,2880]{2,1,0:T(8,128)(2,1)}, u32[]{:S(2)}, u32[]{:S(2)}) async-start(bf16[128,6,2880]{2,1,0:T(8,128)(2,1)} %reshape.822), calls=%async_computation.2 | async-start | bytes 12058624 | tf_op jit(solution)/shard_map/all_to_all | solution.py:207
  237.6 0.2 select_reduce_fusion.1
  237.8 0.1 copy.84
  237.9 0.1 reshape.841
  238.1 0.1 fusion.37
  238.3 1.0 scatter_fusion
  239.3 71.2 %all-to-all-done.1 = bf16[128,6,2880]{2,1,0:T(8,128)(2,1)} async-done(((bf16[128,6,2880]{2,1,0:T(8,128)(2,1)}), bf16[128,6,2880]{2,1,0:T(8,128)(2,1)}, u32[]{:S(2)}, u32[]{:S(2)}) %all-to-all-start.1) | async-done | bytes 4423712 | tf_op jit(solution)/shard_map/all_to_all | solution.py:207
  310.5 6.0 %convert_reduce_fusion = f32[32,6,2880]{2,1,0:T(8,128)} fusion(bf16[128,6,2880]{2,1,0:T(8,128)(2,1)} %all-to-all-done.1), kind=kLoop, calls=%fused_computation.4 | loop fusion | flops 3870720 | bytes 6635520 | tf_op jit(solution)/shard_map/reduce_sum | solution.py:120
  316.5 3.0 reshape.825
  319.5 4.6 %gather_fusion.1 = f32[128,2880]{1,0:T(8,128)} fusion(f32[192,2880]{1,0:T(8,128)} %reshape.825, s32[1024]{0:T(1024)S(1)} %pad_clamp_fusion.1), kind=kCustom, calls=%fused_computation.1 | custom fusion | bytes 2949632 | tf_op jit(solution)/shard_map/gather | solution.py:213
  324.1 2.8 reshape.840
  326.9 2.4 multiply_reduce_fusion
  329.4 0.7 add_convert_fusion
  (85 shorter events, 1.6 us)
Async XLA Ops:
  7.2 49.2 %copy-start = (bf16[512,2880]{0,1:T(8,128)(2,1)S(1)}, bf16[512,2880]{0,1:T(8,128)(2,1)}, u32[]{:S(2)}) copy-start(bf16[512,2880]{0,1:T(8,128)(2,1)} %param.17) | copy-start | bytes 8847364
  7.2 29.8 %all-gather.2.cloned.1.call-start = ((), (), s32[]{:S(2)}) async-start(), calls=%async_computation.4 | async-start | bytes 1695744 | tf_op jit(solution)/shard_map/all_gather | solution.py:158
  10.2 81.3 %reduce-scatter.2.cloned.1.call-start = ((), (), s32[]{:S(2)}) async-start(), calls=%async_computation.5 | async-start | bytes 1695744 | tf_op jit(solution)/shard_map/reduce_scatter | solution.py:182
  12.3 0.5 copy-start.12
  36.9 8.4 %copy-start.7 = (f32[256,32]{0,1:T(8,128)S(1)}, f32[256,32]{0,1:T(8,128)}, u32[]{:S(2)}) copy-start(f32[256,32]{0,1:T(8,128)} %get-tuple-element.12) | copy-start | bytes 98308
  36.9 8.4 %copy-start.8 = (f32[256,32]{0,1:T(8,128)S(1)}, f32[256,32]{0,1:T(8,128)}, u32[]{:S(2)}) copy-start(f32[256,32]{0,1:T(8,128)} %get-tuple-element.13) | copy-start | bytes 98308
  41.9 10.2 %collective-permute-start = (bf16[128,1,128]{0,2,1:T(8,128)(2,1)}, bf16[128,1,128]{0,2,1:T(8,128)(2,1)}, u32[]{:S(2)}, u32[]{:S(2)}) collective-permute-start(bf16[128,1,128]{0,2,1:T(8,128)(2,1)} %pad_maximum_fusion.3), channel_id=1, source_target_pairs={{0,8},{8,16},{16,24},{24,32},{32,40},{40,48},{48,56},{56,64},{64,7... | collective-permute-start | bytes 98312 | tf_op jit(solution)/shard_map/ppermute | solution.py:25
  52.1 3.4 %copy-start.5 = (pred[2,128,256]{1,2,0:T(8,128)(4,1)S(1)}, pred[2,128,256]{1,2,0:T(8,128)(4,1)}, u32[]{:S(2)}) copy-start(pred[2,128,256]{1,2,0:T(8,128)(4,1)} %fusion.22) | copy-start | bytes 196612
  52.9 2.5 copy-start.15
  56.3 2.3 copy-start.13
  56.3 2.4 copy-start.9
  56.4 35.2 %copy-start.2 = (bf16[32,2880]{1,0:T(8,128)(2,1)S(1)}, bf16[32,2880]{1,0:T(8,128)(2,1)}, u32[]{:S(2)}) copy-start(bf16[32,2880]{1,0:T(8,128)(2,1)} %param.12) | copy-start | bytes 552964
  56.4 36.3 %copy-start.10 = (f32[2880]{0:T(1024)S(1)}, f32[2880]{0:T(1024)}, u32[]{:S(2)}) copy-start(f32[2880]{0:T(1024)} %param.18) | copy-start | bytes 34564
  101.0 7.4 %copy-start.11 = (s32[256]{0:T(256)S(1)}, s32[256]{0:T(256)}, u32[]{:S(2)}) copy-start(s32[256]{0:T(256)} %param.23) | copy-start | bytes 3076
  101.1 8.3 %copy-start.4 = (bf16[256,1,1,64]{0,3,2,1:T(8,128)(2,1)S(1)}, bf16[256,1,1,64]{0,3,2,1:T(8,128)(2,1)}, u32[]{:S(2)}) copy-start(bf16[256,1,1,64]{0,3,2,1:T(8,128)(2,1)} %slice.143) | copy-start | bytes 98308
  101.1 80.4 %all-to-all-start = ((bf16[128,6,2880]{2,1,0:T(8,128)(2,1)}), bf16[128,6,2880]{2,1,0:T(8,128)(2,1)}, u32[]{:S(2)}, u32[]{:S(2)}) async-start(bf16[128,6,2880]{2,1,0:T(8,128)(2,1)} %bitcast.119), calls=%async_computation.1 | async-start | bytes 12058624 | tf_op jit(solution)/shard_map/all_to_all | solution.py:207
  181.5 48.6 %all-to-all-start.2 = ((bf16[16,1,16,1,128]{4,2,3,1,0:T(8,128)(2,1)}), bf16[16,1,16,1,128]{4,2,3,1,0:T(8,128)(2,1)S(1)}, u32[]{:S(2)}, u32[]{:S(2)}) async-start(bf16[16,1,16,1,128]{4,2,3,1,0:T(8,128)(2,1)} %bitcast.37), calls=%async_computation.3 | async-start | bytes 131072 | tf_op jit(solution)/shard_map/all_to_all | solution.py:228
  230.1 7.9 %copy-start.14 = (f32[32,4]{0,1:T(4,128)S(1)}, f32[32,4]{0,1:T(4,128)}, u32[]{:S(2)}) copy-start(f32[32,4]{0,1:T(4,128)} %param.20) | copy-start | bytes 1540
  230.1 80.4 %all-to-all-start.1 = ((bf16[128,6,2880]{2,1,0:T(8,128)(2,1)}), bf16[128,6,2880]{2,1,0:T(8,128)(2,1)}, u32[]{:S(2)}, u32[]{:S(2)}) async-start(bf16[128,6,2880]{2,1,0:T(8,128)(2,1)} %reshape.822), calls=%async_computation.2 | async-start | bytes 12058624 | tf_op jit(solution)/shard_map/all_to_all | solution.py:207
  239.3 77.2 %copy-start.6 = (bf16[16,16,128]{2,1,0:T(8,128)(2,1)}, bf16[16,16,128]{2,1,0:T(8,128)(2,1)S(1)}, u32[]{:S(2)}) copy-start(bf16[16,16,128]{2,1,0:T(8,128)(2,1)S(1)} %scatter_fusion) | copy-start | bytes 196612
  319.5 10.6 %copy-start.1 = (bf16[512,2880]{0,1:T(8,128)(2,1)S(1)}, bf16[512,2880]{0,1:T(8,128)(2,1)}, u32[]{:S(2)}) copy-start(bf16[512,2880]{0,1:T(8,128)(2,1)} %param.17) | copy-start | bytes 8847364
  324.1 5.2 %copy-start.3 = (bf16[32,2880]{1,0:T(8,128)(2,1)S(1)}, bf16[32,2880]{1,0:T(8,128)(2,1)}, u32[]{:S(2)}) copy-start(bf16[32,2880]{1,0:T(8,128)(2,1)} %reduce-scatter.2.cloned.1.call-done) | copy-start | bytes 552964
Sparse Core Ops, SparseCore 0:
  10.3 26.5 all-gather.1
  58.7 32.7 reduce-scatter.1
where the time goes:
time: 339 us; the launch traced here: 337 us
  waiting for transfers between devices  196 us (58%)
  local copies, waits for them, and re-layouts  50.4 us (15%)
  matrix products  27.2 us (8%)
  starting transfers between devices  25.7 us (8%)
  other arithmetic  22.7 us (7%)
  between operations  14.5 us (4%)
    all_to_all x2, waiting for transfers between devices, flat_route(): lax.all_to_all(blocks, ('tok', 'head'), split_axis=0, concat_axis=0, tile...  142 us
    reduce_scatter x1, waiting for transfers between devices, per_device(): lax.psum_scatter(jnp.dot(attended, w_out_attn, preferred_element_type=jnp...  32.2 us
    all_gather x1, waiting for transfers between devices, per_device(): lax.all_gather(normed_input, 'head', axis=0, tiled=True)  22.3 us
    all_to_all x2, starting transfers between devices, flat_route(): lax.all_to_all(blocks, ('tok', 'head'), split_axis=0, concat_axis=0, tile...  14.8 us
    dot_general x1, matrix products, expert_mlp(): gate_up = jnp.dot(rows_in, w_in_local, preferred_element_type=jnp.float32)  10.8 us
    reshape x1, local copies, waits for them, and re-layouts, copied_route(): incoming.reshape(-1, MODEL_WIDTH)  8.18 us
    dot_general x1, matrix products, expert_mlp(): jnp.dot(activated, w_down_local, preferred_element_type=jnp.float32)  8.09 us
    reshape x1, local copies, waits for them, and re-layouts, copied_route(): expert_mlp(incoming.reshape(-1, MODEL_WIDTH), w_in_local, w_down_local)  7.59 us
  transfers between devices with their start and end apart: 6, of which 4 were waited for; matrix products, arithmetic and copies ran while one was open for 17% of the time, Pallas kernels for 0%

commit v1 on v0

--- a/solution.py
+++ b/solution.py
@@ -1,8 +1,11 @@
+import functools
 import math
 
 import jax
 import jax.numpy as jnp
 from jax import lax
+from jax.experimental import pallas as pl
+from jax.experimental.pallas import tpu as pltpu
 from jax.sharding import PartitionSpec as P
 
 MODEL_WIDTH = 2880
@@ -97,29 +100,584 @@
     )
 
 
-def expert_mlp(rows_in, w_in_local, w_down_local):
-    ffs_local = w_down_local.shape[0]
-    gate_up = jnp.dot(rows_in, w_in_local, preferred_element_type=jnp.float32)
-    gate_part = gate_up[:, :ffs_local]
-    up_part = gate_up[:, ffs_local:]
-    activated = ((up_part + 1.0) * gate_part * jax.nn.sigmoid(GLU_ALPHA * gate_part)).astype(
-        jnp.bfloat16
-    )
-    return jnp.dot(activated, w_down_local, preferred_element_type=jnp.float32).astype(jnp.bfloat16)
-
-
-def copied_route(outgoing, route, width_split, slots, w_in_local, w_down_local):
-    spread = jnp.broadcast_to(
-        outgoing[:, None], (EXPERTS, width_split, slots, MODEL_WIDTH)
-    ).reshape(EXPERTS * width_split, slots, MODEL_WIDTH)
-    incoming = route(spread)
-    produced = expert_mlp(incoming.reshape(-1, MODEL_WIDTH), w_in_local, w_down_local).reshape(
-        spread.shape
-    )
-    returned = route(produced)
-    return jnp.sum(
-        returned.astype(jnp.float32).reshape(EXPERTS, width_split, slots, MODEL_WIDTH), axis=1
-    ).reshape(EXPERTS * slots, MODEL_WIDTH)
+MESH = pl.DeviceIdType.MESH
+VM = pltpu.VMEM
+CHIPS = 64
+ROWS = 32
+SLOTS = 6
+PARTS = 4
+PART_WIDTH = MODEL_WIDTH // PARTS
+CHUNK = PARTS * SLOTS
+HEADS = 8
+
+
+def vmem_spec():
+    return pl.BlockSpec(memory_space=pltpu.VMEM)
+
+
+def any_spec():
+    return pl.BlockSpec(memory_space=pl.ANY)
+
+
+def place():
+    tok = lax.axis_index("tok")
+    head = lax.axis_index("head")
+    return (tok // 4, head // 2, tok % 4, head % 2)
+
+
+def device(x, y, z, core):
+    return (x * 4 + z, y * 2 + core)
+
+
+def shifted(k, sign):
+    x, y, z, core = place()
+    dx, dy, dz = k // 16, (k // 4) % 4, k % 4
+    if sign < 0:
+        dx, dy, dz = 4 - dx, 4 - dy, 4 - dz
+    return ((x + dx) % 4, (y + dy) % 4, (z + dz) % 4, core)
+
+
+def sibling():
+    x, y, z, core = place()
+    return device(x, y, z, 1 - core)
+
+
+def signal(barrier, target):
+    pl.semaphore_signal(barrier, inc=1, device_id=target, device_id_type=MESH)
+
+
+def greet_all(barrier):
+    def greet(k, carry):
+        signal(barrier, device(*shifted(k, 1)))
+        return carry
+
+    lax.fori_loop(1, CHIPS, greet, 0)
+    signal(barrier, sibling())
+
+
+def remote(src, dst, send, recv, target):
+    return pltpu.make_async_remote_copy(
+        src_ref=src, dst_ref=dst, send_sem=send, recv_sem=recv, device_id=target, device_id_type=MESH
+    )
+
+
+def gather_kernel(rows_ref, out_ref, send, recv, fsend, frecv, local):
+    x, y, z, core = place()
+    barrier = pltpu.get_barrier_semaphore()
+    up = device(x, (y + 1) % 4, z, core)
+    down = device(x, (y + 3) % 4, z, core)
+    sib = sibling()
+    for target in (up, down, sib):
+        signal(barrier, target)
+    pl.semaphore_wait(barrier, 3)
+    mine = y * 2 + core
+    lower = ((y + 3) % 4) * 2 + core
+    upper = ((y + 1) % 4) * 2 + core
+    far = ((y + 2) % 4) * 2 + core
+    half = ROWS // 2
+    first = pl.ds(0, half)
+    second = pl.ds(half, half)
+    to_up = remote(rows_ref, out_ref.at[mine], send.at[0], recv.at[0], up)
+    to_down = remote(rows_ref, out_ref.at[mine], send.at[1], recv.at[1], down)
+    to_sib = remote(rows_ref, out_ref.at[mine], fsend.at[0], frecv.at[0], sib)
+    keep = pltpu.make_async_copy(rows_ref, out_ref.at[mine], local)
+    to_up.start()
+    to_down.start()
+    to_sib.start()
+    keep.start()
+    to_up.wait_recv()
+    on_up = remote(
+        out_ref.at[lower, first], out_ref.at[lower, first], send.at[2], recv.at[2], up
+    )
+    on_up.start()
+    sib_low = remote(out_ref.at[lower], out_ref.at[lower], fsend.at[1], frecv.at[1], sib)
+    sib_low.start()
+    to_down.wait_recv()
+    on_down = remote(
+        out_ref.at[upper, second], out_ref.at[upper, second], send.at[3], recv.at[3], down
+    )
+    on_down.start()
+    sib_up = remote(out_ref.at[upper], out_ref.at[upper], fsend.at[2], frecv.at[2], sib)
+    sib_up.start()
+    on_up.wait_recv()
+    on_down.wait_recv()
+    sib_far = remote(out_ref.at[far], out_ref.at[far], fsend.at[3], frecv.at[3], sib)
+    sib_far.start()
+    for copy in (to_sib, sib_low, sib_up, sib_far):
+        copy.wait()
+    for copy in (to_up, to_down, on_up, on_down):
+        copy.wait_send()
+    keep.wait()
+
+
+def gather_rows(rows):
+    out = pl.pallas_call(
+        gather_kernel,
+        out_shape=jax.ShapeDtypeStruct((HEADS, ROWS, MODEL_WIDTH), jnp.bfloat16),
+        in_specs=[vmem_spec()],
+        out_specs=any_spec(),
+        scratch_shapes=[
+            pltpu.SemaphoreType.DMA((4,)),
+            pltpu.SemaphoreType.DMA((4,)),
+            pltpu.SemaphoreType.DMA((4,)),
+            pltpu.SemaphoreType.DMA((4,)),
+            pltpu.SemaphoreType.DMA,
+        ],
+        compiler_params=pltpu.CompilerParams(collective_id=0, has_side_effects=True),
+        name="gather_rows",
+    )(rows)
+    return out.reshape(HEADS * ROWS, MODEL_WIDTH)
+
+
+def reduce_kernel(part_ref, out_ref, pair_buf, sums, far_buf, psend, precv, send, recv):
+    x, y, z, core = place()
+    barrier = pltpu.get_barrier_semaphore()
+    sib = sibling()
+    signal(barrier, sib)
+    for step in range(1, 4):
+        signal(barrier, device(x, (y + step) % 4, z, core))
+    pl.semaphore_wait(barrier, 4)
+    order = (1, 2, 3, 0)
+    pairs = []
+    for step in order:
+        owner = (y + step) % 4
+        copy = remote(
+            part_ref.at[owner * 2 + 1 - core], pair_buf.at[step], psend.at[step], precv.at[step], sib
+        )
+        copy.start()
+        pairs.append(copy)
+    sent = []
+    for index, step in enumerate(order):
+        owner = (y + step) % 4
+        pairs[index].wait_recv()
+        total = part_ref[owner * 2 + core].astype(jnp.float32) + pair_buf[step].astype(jnp.float32)
+        if step == 0:
+            own_sum = total
+        else:
+            sums[step] = total.astype(jnp.bfloat16)
+        if index > 0:
+            before = order[index - 1]
+            copy = remote(
+                sums.at[before],
+                far_buf.at[before],
+                send.at[before],
+                recv.at[before],
+                device(x, (y + before) % 4, z, core),
+            )
+            copy.start()
+            sent.append(copy)
+    for copy in sent:
+        copy.wait_recv()
+    for step in range(1, 4):
+        own_sum = own_sum + far_buf[step].astype(jnp.float32)
+    out_ref[...] = own_sum
+    for copy in pairs + sent:
+        copy.wait_send()
+
+
+def sum_over_heads(part):
+    return pl.pallas_call(
+        reduce_kernel,
+        out_shape=jax.ShapeDtypeStruct((ROWS, MODEL_WIDTH), jnp.float32),
+        in_specs=[vmem_spec()],
+        out_specs=vmem_spec(),
+        scratch_shapes=[
+            VM((4, ROWS, MODEL_WIDTH), jnp.bfloat16),
+            VM((4, ROWS, MODEL_WIDTH), jnp.bfloat16),
+            VM((4, ROWS, MODEL_WIDTH), jnp.bfloat16),
+            pltpu.SemaphoreType.DMA((4,)),
+            pltpu.SemaphoreType.DMA((4,)),
+            pltpu.SemaphoreType.DMA((4,)),
+            pltpu.SemaphoreType.DMA((4,)),
+        ],
+        compiler_params=pltpu.CompilerParams(collective_id=1, has_side_effects=True),
+        name="sum_over_heads",
+    )(part.reshape(HEADS, ROWS, MODEL_WIDTH))
+
+
+def iota(shape, dim):
+    return lax.broadcasted_iota(jnp.int32, shape, dim)
+
+
+def split_index(index, size):
+    whole = jnp.floor((index.astype(jnp.float32) + 0.5) * (1.0 / size)).astype(jnp.int32)
+    return (whole, index - whole * size)
+
+
+def prepare_kernel(sum_ref, tok_ref, gain_ref, routes_ref, live_ref, resid_ref, out_ref):
+    resid = tok_ref[...].astype(jnp.float32) + sum_ref[...]
+    resid_ref[...] = resid
+    inv_rms = lax.rsqrt(jnp.mean(resid * resid, axis=-1, keepdims=True) + EPSILON)
+    moe_in = (resid * inv_rms * gain_ref[...]).astype(jnp.bfloat16)
+    expert = iota((EXPERTS, ROWS), 0)
+    routed = jnp.zeros((EXPERTS, ROWS), jnp.float32)
+    for k in range(4):
+        routed = routed + jnp.where(routes_ref[k : k + 1, :] == expert, 1.0, 0.0)
+    routed = routed * live_ref[0:1, :ROWS]
+    earlier = jnp.where(iota((ROWS, ROWS), 0) < iota((ROWS, ROWS), 1), 1.0, 0.0)
+    rank = jnp.dot(
+        routed.astype(jnp.bfloat16), earlier.astype(jnp.bfloat16), preferred_element_type=jnp.float32
+    )
+    code = jnp.where(routed > 0.5, rank, -1.0).astype(jnp.bfloat16)
+    count = EXPERTS * CHUNK
+    owner, within = split_index(iota((count, EXPERTS), 0), CHUNK)
+    spread = jnp.where(owner == iota((count, EXPERTS), 1), 1.0, 0.0).astype(jnp.bfloat16)
+    code_rows = jnp.dot(spread, code, preferred_element_type=jnp.float32)
+    _, within = split_index(iota((count, ROWS), 0), CHUNK)
+    part, slot = split_index(within, SLOTS)
+    hit = jnp.abs(code_rows - slot.astype(jnp.float32)) < 0.5
+    total = jnp.zeros((count, PART_WIDTH), jnp.float32)
+    for q in range(PARTS):
+        pick = jnp.where(hit & (part == q), 1.0, 0.0).astype(jnp.bfloat16)
+        total = total + jnp.dot(
+            pick, moe_in[:, q * PART_WIDTH : (q + 1) * PART_WIDTH], preferred_element_type=jnp.float32
+        )
+    out_ref[...] = total.astype(jnp.bfloat16)
+
+
+def prepare_chunks(attn_sum, tokens, gain, routes_t, live_row):
+    resid, out = pl.pallas_call(
+        prepare_kernel,
+        out_shape=(
+            jax.ShapeDtypeStruct((ROWS, MODEL_WIDTH), jnp.float32),
+            jax.ShapeDtypeStruct((EXPERTS * CHUNK, PART_WIDTH), jnp.bfloat16),
+        ),
+        in_specs=[vmem_spec()] * 5,
+        out_specs=(vmem_spec(), vmem_spec()),
+        name="prepare_chunks",
+    )(attn_sum, tokens, gain.reshape(1, MODEL_WIDTH), routes_t, live_row)
+    return (resid, out.reshape(EXPERTS, CHUNK, PART_WIDTH))
+
+
+def dispatch_kernel(
+    out_ref, pages_ref, recv_ref, arrived_ref, send, recv, fsend, frecv, psend, precv, local
+):
+    x, y, z, core = place()
+    tok = x * 4 + z
+    barrier = pltpu.get_barrier_semaphore()
+    sib = sibling()
+    greet_all(barrier)
+    pl.semaphore_wait(barrier, CHIPS)
+
+    def chunk(k):
+        tx, ty, tz, tc = shifted(k, 1)
+        expert = (tx * 4 + tz) * 2 + ty // 2
+        return remote(
+            out_ref.at[expert], recv_ref.at[0, k], send.at[k], recv.at[k], device(tx, ty, tz, tc)
+        )
+
+    def page(j):
+        tx, tz = (x + j // 4) % 4, (z + j % 4) % 4
+        return remote(
+            pages_ref.at[tx * 4 + tz],
+            arrived_ref.at[tok],
+            psend.at[j],
+            precv.at[j],
+            device(tx, y, tz, core),
+        )
+
+    def start_chunk(k, carry):
+        chunk(k).start()
+        return carry
+
+    def start_page(j, carry):
+        page(j).start()
+        return carry
+
+    lax.fori_loop(1, CHIPS, start_chunk, 0)
+    own = pltpu.make_async_copy(out_ref.at[tok * 2 + y // 2], recv_ref.at[0, 0], local.at[0])
+    own.start()
+    own_page = pltpu.make_async_copy(pages_ref.at[tok], arrived_ref.at[tok], local.at[1])
+    own_page.start()
+    lax.fori_loop(1, 16, start_page, 0)
+    own.wait()
+
+    def forward(g):
+        block = pl.ds(g * 8, 8)
+        return remote(recv_ref.at[0, block], recv_ref.at[1, block], fsend.at[g], frecv.at[g], sib)
+
+    def arrive(k, carry):
+        chunk(k).wait_recv()
+        return carry
+
+    def pass_on(g, carry):
+        lax.fori_loop(jnp.maximum(g * 8, 1), g * 8 + 8, arrive, 0)
+        forward(g).start()
+        return carry
+
+    lax.fori_loop(0, 8, pass_on, 0)
+
+    def finish_forward(g, carry):
+        forward(g).wait()
+        return carry
+
+    def finish_chunk(k, carry):
+        chunk(k).wait_send()
+        return carry
+
+    def finish_page(j, carry):
+        page(j).wait()
+        return carry
+
+    lax.fori_loop(0, 8, finish_forward, 0)
+    lax.fori_loop(1, CHIPS, finish_chunk, 0)
+    lax.fori_loop(1, 16, finish_page, 0)
+    own_page.wait()
+
+
+def dispatch(outgoing, pages):
+    return pl.pallas_call(
+        dispatch_kernel,
+        out_shape=(
+            jax.ShapeDtypeStruct((2, CHIPS, CHUNK, PART_WIDTH), jnp.bfloat16),
+            jax.ShapeDtypeStruct((16, PAGE_TOKENS, 2 * HEAD_SIZE), jnp.bfloat16),
+        ),
+        in_specs=[vmem_spec(), vmem_spec()],
+        out_specs=(any_spec(), any_spec()),
+        scratch_shapes=[
+            pltpu.SemaphoreType.DMA((CHIPS,)),
+            pltpu.SemaphoreType.DMA((CHIPS,)),
+            pltpu.SemaphoreType.DMA((8,)),
+            pltpu.SemaphoreType.DMA((8,)),
+            pltpu.SemaphoreType.DMA((16,)),
+            pltpu.SemaphoreType.DMA((16,)),
+            pltpu.SemaphoreType.DMA((2,)),
+        ],
+        compiler_params=pltpu.CompilerParams(collective_id=2, has_side_effects=True),
+        name="dispatch",
+    )(outgoing, pages)
+
+
+GROUPS = 8
+GROUP_ROWS = 2 * CHIPS * CHUNK // GROUPS
+GROUP_SLOTS = GROUP_ROWS // PARTS
+EXPERT_ROWS = GROUPS * GROUP_SLOTS
+DOT_ROWS = 256
+
+
+def expert_kernel(recv_ref, win_ref, wdown_ref, y_ref, rbuf, w1, w2, xs, acc, ys, sem):
+    copies_r = [
+        pltpu.make_async_copy(recv_ref.at[b], rbuf.at[b], sem.at[b]) for b in range(GROUPS)
+    ]
+    copies_w = [
+        pltpu.make_async_copy(
+            win_ref.at[pl.ds(q * PART_WIDTH, PART_WIDTH)], w1.at[q], sem.at[GROUPS + q]
+        )
+        for q in range(PARTS)
+    ]
+    copy_d = pltpu.make_async_copy(wdown_ref, w2, sem.at[GROUPS + PARTS])
+    for copy in copies_r + copies_w + [copy_d]:
+        copy.start()
+    shape = (GROUP_ROWS, GROUP_ROWS)
+    part, row = split_index(iota(shape, 0), GROUP_SLOTS)
+    row_source, row_slot = split_index(row, SLOTS)
+    col_source, col = split_index(iota(shape, 1), CHUNK)
+    col_part, col_slot = split_index(col, SLOTS)
+    match = (part == col_part) & (row_source == col_source) & (row_slot == col_slot)
+    perm = jnp.where(match, 1.0, 0.0).astype(jnp.bfloat16)
+    part, row = split_index(iota(shape, 1), GROUP_SLOTS)
+    row_source, row_slot = split_index(row, SLOTS)
+    col_source, col = split_index(iota(shape, 0), CHUNK)
+    col_part, col_slot = split_index(col, SLOTS)
+    match = (part == col_part) & (row_source == col_source) & (row_slot == col_slot)
+    back = jnp.where(match, 1.0, 0.0).astype(jnp.bfloat16)
+    for copy in copies_r:
+        copy.wait()
+
+    def sort_in(b, carry):
+        mixed = jnp.dot(perm, rbuf[b], preferred_element_type=jnp.float32).astype(jnp.bfloat16)
+        start = pl.multiple_of(b * GROUP_SLOTS, GROUP_SLOTS)
+        for q in range(PARTS):
+            xs[q, pl.ds(start, GROUP_SLOTS), :] = mixed[q * GROUP_SLOTS : (q + 1) * GROUP_SLOTS]
+        return carry
+
+    lax.fori_loop(0, GROUPS, sort_in, 0)
+    for copy in copies_w:
+        copy.wait()
+
+    def up_block(i, carry):
+        rows = pl.ds(pl.multiple_of(i * DOT_ROWS, DOT_ROWS), DOT_ROWS)
+        acc[...] = jnp.dot(xs[0, rows, :], w1[0], preferred_element_type=jnp.float32)
+        for q in range(1, PARTS):
+            acc[...] += jnp.dot(xs[q, rows, :], w1[q], preferred_element_type=jnp.float32)
+        gate = acc[:, :PART_WIDTH]
+        up = acc[:, PART_WIDTH:]
+        act = (up + 1.0) * gate * jax.nn.sigmoid(GLU_ALPHA * gate)
+        xs[0, rows, :] = act.astype(jnp.bfloat16)
+        return carry
+
+    lax.fori_loop(0, EXPERT_ROWS // DOT_ROWS, up_block, 0)
+    copy_d.wait()
+
+    def down_block(i, carry):
+        rows = pl.ds(pl.multiple_of(i * DOT_ROWS, DOT_ROWS), DOT_ROWS)
+        down = jnp.dot(xs[0, rows, :], w2[...], preferred_element_type=jnp.float32)
+        down = down.astype(jnp.bfloat16)
+        for q in range(PARTS):
+            ys[q, rows, :] = down[:, q * PART_WIDTH : (q + 1) * PART_WIDTH]
+        return carry
+
+    lax.fori_loop(0, EXPERT_ROWS // DOT_ROWS, down_block, 0)
+
+    def sort_out(b, carry):
+        rows = pl.ds(pl.multiple_of(b * GROUP_SLOTS, GROUP_SLOTS), GROUP_SLOTS)
+        total = jnp.zeros((GROUP_ROWS, PART_WIDTH), jnp.float32)
+        stacked = jnp.concatenate([ys[q, rows, :] for q in range(PARTS)], axis=0)
+        y_ref[b] = jnp.dot(back, stacked, preferred_element_type=jnp.float32).astype(jnp.bfloat16)
+        return carry
+
+    lax.fori_loop(0, GROUPS, sort_out, 0)
+
+
+def run_experts(received, w_in, w_down):
+    out = pl.pallas_call(
+        expert_kernel,
+        out_shape=jax.ShapeDtypeStruct((GROUPS, GROUP_ROWS, PART_WIDTH), jnp.bfloat16),
+        in_specs=[any_spec()] * 3,
+        out_specs=vmem_spec(),
+        scratch_shapes=[
+            VM((GROUPS, GROUP_ROWS, PART_WIDTH), jnp.bfloat16),
+            VM((PARTS, PART_WIDTH, 2 * PART_WIDTH), jnp.bfloat16),
+            VM((PART_WIDTH, MODEL_WIDTH), jnp.bfloat16),
+            VM((PARTS, EXPERT_ROWS, PART_WIDTH), jnp.bfloat16),
+            VM((DOT_ROWS, 2 * PART_WIDTH), jnp.float32),
+            VM((PARTS, EXPERT_ROWS, PART_WIDTH), jnp.bfloat16),
+            pltpu.SemaphoreType.DMA((GROUPS + PARTS + 1,)),
+        ],
+        compiler_params=pltpu.CompilerParams(vmem_limit_bytes=60 << 20),
+        name="run_experts",
+    )(received.reshape(GROUPS, GROUP_ROWS, PART_WIDTH), w_in, w_down)
+    return out.reshape(2, CHIPS, CHUNK, PART_WIDTH)
+
+
+def return_kernel(y_ref, ret_ref, own, pair, sums, psend, precv, send, recv, lsem, last):
+    barrier = pltpu.get_barrier_semaphore()
+    sib = sibling()
+    greet_all(barrier)
+
+    def load(g):
+        block = pl.ds(g * 8, 8)
+        return pltpu.make_async_copy(y_ref.at[0, block], own.at[block], lsem.at[g])
+
+    def start_load(g, carry):
+        load(g).start()
+        return carry
+
+    lax.fori_loop(0, 8, start_load, 0)
+    pl.semaphore_wait(barrier, CHIPS)
+
+    def exchange(g):
+        block = pl.ds(g * 8, 8)
+        return remote(y_ref.at[1, block], pair.at[block], psend.at[g], precv.at[g], sib)
+
+    def start_exchange(g, carry):
+        exchange(g).start()
+        return carry
+
+    lax.fori_loop(0, 8, start_exchange, 0)
+
+    def chunk(k):
+        return remote(
+            sums.at[k], ret_ref.at[k], send.at[k], recv.at[k], device(*shifted(k, -1))
+        )
+
+    def start_chunk(k, carry):
+        chunk(k).start()
+        return carry
+
+    def add(g, carry):
+        exchange(g).wait_recv()
+        load(g).wait()
+        block = pl.ds(g * 8, 8)
+        sums[block] = (own[block].astype(jnp.float32) + pair[block].astype(jnp.float32)).astype(
+            jnp.bfloat16
+        )
+        lax.fori_loop(jnp.maximum((g - 1) * 8, 1), g * 8, start_chunk, 0)
+        return carry
+
+    lax.fori_loop(0, 8, add, 0)
+    home = pltpu.make_async_copy(sums.at[0], ret_ref.at[0], last)
+    home.start()
+    lax.fori_loop(CHIPS - 8, CHIPS, start_chunk, 0)
+
+    def finish_exchange(g, carry):
+        exchange(g).wait_send()
+        return carry
+
+    def finish_chunk(k, carry):
+        chunk(k).wait()
+        return carry
+
+    lax.fori_loop(0, 8, finish_exchange, 0)
+    lax.fori_loop(1, CHIPS, finish_chunk, 0)
+    home.wait()
+
+
+def give_back(y):
+    return pl.pallas_call(
+        return_kernel,
+        out_shape=jax.ShapeDtypeStruct((CHIPS, CHUNK, PART_WIDTH), jnp.bfloat16),
+        in_specs=[any_spec()],
+        out_specs=any_spec(),
+        scratch_shapes=[
+            VM((CHIPS, CHUNK, PART_WIDTH), jnp.bfloat16),
+            VM((CHIPS, CHUNK, PART_WIDTH), jnp.bfloat16),
+            VM((CHIPS, CHUNK, PART_WIDTH), jnp.bfloat16),
+            pltpu.SemaphoreType.DMA((8,)),
+            pltpu.SemaphoreType.DMA((8,)),
+            pltpu.SemaphoreType.DMA((CHIPS,)),
+            pltpu.SemaphoreType.DMA((CHIPS,)),
+            pltpu.SemaphoreType.DMA((8,)),
+            pltpu.SemaphoreType.DMA,
+        ],
+        compiler_params=pltpu.CompilerParams(collective_id=3, has_side_effects=True),
+        name="give_back",
+    )(y)
+
+
+def combine_kernel(ret_ref, resid_ref, routes_ref, gates_ref, live_ref, home_ref, out_ref):
+    expert = iota((ROWS, EXPERTS), 1)
+    routed = jnp.zeros((ROWS, EXPERTS), jnp.float32)
+    gate = jnp.zeros((ROWS, EXPERTS), jnp.float32)
+    for k in range(4):
+        named = routes_ref[:, k : k + 1] == expert
+        routed = routed + jnp.where(named, 1.0, 0.0)
+        gate = gate + jnp.where(named, gates_ref[:, k : k + 1], 0.0)
+    routed = routed * live_ref[0:1, :EXPERTS]
+    earlier = jnp.where(iota((ROWS, ROWS), 1) < iota((ROWS, ROWS), 0), 1.0, 0.0)
+    rank = jnp.dot(
+        earlier.astype(jnp.bfloat16), routed.astype(jnp.bfloat16), preferred_element_type=jnp.float32
+    )
+    code = jnp.where(routed > 0.5, rank, -1.0).astype(jnp.bfloat16)
+    count = CHIPS * CHUNK
+    spread = jnp.where(iota((EXPERTS, count), 0) == home_ref[...], 1.0, 0.0).astype(jnp.bfloat16)
+    code_cols = jnp.dot(code, spread, preferred_element_type=jnp.float32)
+    gate_cols = jnp.dot(gate.astype(jnp.bfloat16), spread, preferred_element_type=jnp.float32)
+    _, within = split_index(iota((ROWS, count), 1), CHUNK)
+    part, slot = split_index(within, SLOTS)
+    weight = jnp.where(jnp.abs(code_cols - slot.astype(jnp.float32)) < 0.5, gate_cols, 0.0)
+    stacked = jnp.concatenate(
+        [jnp.where(part == q, weight, 0.0).astype(jnp.bfloat16) for q in range(PARTS)], axis=0
+    )
+    total = jnp.dot(stacked, ret_ref[...], preferred_element_type=jnp.float32)
+    for q in range(PARTS):
+        cols = slice(q * PART_WIDTH, (q + 1) * PART_WIDTH)
+        out_ref[:, cols] = (
+            resid_ref[:, cols] + total[q * ROWS : (q + 1) * ROWS]
+        ).astype(jnp.bfloat16)
+
+
+def combine(returned, resid, routes, gates, live_row):
+    x, y, z, _ = place()
+    k = jnp.arange(CHIPS * CHUNK, dtype=jnp.int32)[None, :] // CHUNK
+    home = (((x + k // 16) % 4) * 4 + (z + k % 4) % 4) * 2 + ((y + (k // 4) % 4) % 4) // 2
+    return pl.pallas_call(
+        combine_kernel,
+        out_shape=jax.ShapeDtypeStruct((ROWS, MODEL_WIDTH), jnp.bfloat16),
+        in_specs=[vmem_spec()] * 6,
+        out_specs=vmem_spec(),
+        name="combine",
+    )(returned.reshape(CHIPS * CHUNK, PART_WIDTH), resid, routes, gates, live_row, home)
 
 
 def page_order(page_table, n_tok, pages_dev):
@@ -155,7 +713,7 @@
     groups = sinks.shape[0] // QUERY_PER_KEY
     normed_input = normalize(tokens, norm_gain_attn).astype(jnp.bfloat16)
     projected_rows = jnp.dot(
-        lax.all_gather(normed_input, "head", axis=0, tiled=True),
+        gather_rows(normed_input),
         query_key_value_weight,
         preferred_element_type=jnp.float32,
     ).reshape(tok_dev, groups, QUERY_PER_KEY + 2, HEAD_SIZE)
@@ -179,39 +737,12 @@
         sinks.reshape(groups, QUERY_PER_KEY),
         allowed,
     )
-    attn_sum = lax.psum_scatter(
-        jnp.dot(attended, w_out_attn, preferred_element_type=jnp.float32).astype(jnp.bfloat16),
-        "head",
-        scatter_dimension=0,
-        tiled=True,
-    ).astype(jnp.float32)
-    resid = tokens.astype(jnp.float32) + attn_sum
-    moe_in = normalize(resid, norm_gain_moe).astype(jnp.bfloat16)
-    own_index = row_base + head_id * row_count + jnp.arange(row_count, dtype=jnp.int32)
-    own_segs, _ = segment_table(lengths, own_index)
-    is_live = own_segs < NSEQ
-    capacity = row_count // 8 + 2
-    width_split = n_tok * n_head // EXPERTS
-    expert_ids = jnp.arange(EXPERTS, dtype=jnp.int32)
-    naming = routes[:, :, None] == expert_ids[None, None, :]
-    routed = (jnp.any(naming, axis=1) & is_live[:, None]).astype(jnp.int32)
-    slot_rank = jnp.cumsum(routed, axis=0) - 1
-    slot_ids = jnp.arange(capacity, dtype=jnp.int32)
-    placed = (routed == 1)[:, :, None] & (slot_rank[:, :, None] == slot_ids[None, None, :])
-    local_ids = jnp.arange(row_count, dtype=jnp.int32)
-    source_row = jnp.sum(jnp.where(placed, local_ids[:, None, None], 0), axis=0)
-    filled = jnp.any(placed, axis=0)
-    outgoing = jnp.where(filled[:, :, None], moe_in[source_row], jnp.zeros((), jnp.bfloat16))
-
-    def flat_route(blocks):
-        return lax.all_to_all(blocks, ("tok", "head"), split_axis=0, concat_axis=0, tiled=True)
-
-    summed = copied_route(outgoing, flat_route, width_split, capacity, w_in[0], w_down[0])
-    chosen_rank = jnp.sum(jnp.where(naming, slot_rank[:, None, :], 0), axis=2)
-    pick_rows = routes * capacity + jnp.clip(chosen_rank, 0, capacity - 1)
-    weighted = jnp.where(is_live[:, None], gates, 0.0)
-    expert_sum = jnp.sum(summed[pick_rows] * weighted[:, :, None], axis=1)
-    hidden_out = (resid + expert_sum).astype(jnp.bfloat16)
+    attn_sum = sum_over_heads(
+        jnp.dot(attended, w_out_attn, preferred_element_type=jnp.float32).astype(jnp.bfloat16)
+    )
+    live = jnp.where((tok_id * n_head + head_id) * row_count < jnp.sum(lengths), 1.0, 0.0)
+    live_row = jnp.full((1, 128), live, jnp.float32)
+    resid, outgoing = prepare_chunks(attn_sum, tokens, norm_gain_moe, jnp.transpose(routes), live_row)
     pages_dev = tok_dev // PAGE_TOKENS
     share_count = pages_dev // n_tok
     paged = key_value_pairs.reshape(pages_dev, PAGE_TOKENS, groups, 2 * HEAD_SIZE)
@@ -225,7 +756,9 @@
         my_rank[:, None, None] == share_ids[None, None, :]
     )
     pick_page = jnp.sum(jnp.where(matched, page_ids[:, None, None], 0), axis=0)
-    arrived = lax.all_to_all(paged[pick_page], "tok", split_axis=0, concat_axis=0, tiled=True)
+    received, arrived = dispatch(outgoing, paged[pick_page].reshape(n_tok, PAGE_TOKENS, 2 * HEAD_SIZE))
+    returned = give_back(run_experts(received, w_in[0], w_down[0]))
+    hidden_out = combine(returned, resid, routes, gates, live_row)
     to_here = (target == tok_id)[:, :, None] & (order_rank[:, :, None] == share_ids[None, None, :])
     landing = jnp.sum(jnp.where(to_here, slot_grid[:, :, None], 0), axis=1)
     stored = jnp.zeros_like(paged).at[landing.reshape(-1)].set(arrived.reshape(paged.shape))

time: 339 us -> 244 us (0.72)
  waiting for transfers between devices: 196 us -> 0.01 us
  Pallas kernels: 0 us -> 171 us
  starting transfers between devices: 25.7 us -> 3.81 us
  matrix products: 27.2 us -> 7.7 us
  between operations: 14.5 us -> 1.62 us
  local copies, waits for them, and re-layouts: 50.4 us -> 40.9 us
  other arithmetic: 22.7 us -> 16.6 us
    pallas_call x0 -> x7, Pallas kernels: none -> 171 us  [the longest x1 54.4 us: give_back(): pl.pallas_call(return_kernel, out_shape=jax.ShapeDtypeStruct((CHIPS, CHUN...]
    all_to_all x3 -> x0, waiting for transfers between devices: 142 us -> none  [the longest x2 142 us: flat_route(): lax.all_to_all(blocks, ('tok', 'head'), split_axis=0, concat_axis=0, tile...]
    reduce_scatter x1 -> x0, waiting for transfers between devices: 32.2 us -> none  [per_device(): lax.psum_scatter(jnp.dot(attended, w_out_attn, preferred_element_type=jnp...]
    all_gather x1 -> x0, waiting for transfers between devices: 22.3 us -> none  [per_device(): lax.all_gather(normed_input, 'head', axis=0, tiled=True)]
    all_to_all x3 -> x0, starting transfers between devices: 22.2 us -> none  [the longest x2 14.8 us: flat_route(): lax.all_to_all(blocks, ('tok', 'head'), split_axis=0, concat_axis=0, tile...]
    unnamed x32 -> x34, local copies, waits for them, and re-layouts: 0.19 us -> 21.7 us
    dot_general x3 -> x1, matrix products: 23 us -> 3.74 us  [per_device(): jnp.dot(gather_rows(normed_input), query_key_value_weight, preferred_elem...]
    reshape x3 -> x1, local copies, waits for them, and re-layouts: 18.8 us -> 1.31 us  [prepare_chunks(): gain.reshape(1, MODEL_WIDTH)]
  transfers between devices with their start and end apart: 6 -> 1, of which waited for: 4 -> 0; matrix products, arithmetic and copies ran while one was open for 17% -> 17% of each run, Pallas kernels for 0% -> 0%
where the time goes in v1:
time: 244 us; the launch traced here: 242 us
  Pallas kernels  171 us (70%)
  local copies, waits for them, and re-layouts  40.9 us (17%)
  other arithmetic  16.6 us (7%)
  matrix products  7.7 us (3%)
  starting transfers between devices  3.81 us (2%)
    pallas_call x1, Pallas kernels, give_back(): pl.pallas_call(return_kernel, out_shape=jax.ShapeDtypeStruct((CHIPS, CHUN...  54.4 us
    pallas_call x1, Pallas kernels, dispatch(): pl.pallas_call(dispatch_kernel, out_shape=(jax.ShapeDtypeStruct((2, CHIPS...  52.5 us
    pallas_call x1, Pallas kernels, run_experts(): pl.pallas_call(expert_kernel, out_shape=jax.ShapeDtypeStruct((GROUPS, GRO...  25.1 us
    unnamed x34, local copies, waits for them, and re-layouts  21.7 us
    pallas_call x1, Pallas kernels, sum_over_heads(): pl.pallas_call(reduce_kernel, out_shape=jax.ShapeDtypeStruct((ROWS, MODEL...  16.6 us
    pallas_call x1, Pallas kernels, gather_rows(): pl.pallas_call(gather_kernel, out_shape=jax.ShapeDtypeStruct((HEADS, ROWS...  14.9 us
  transfers between devices with their start and end apart: 1, of which 0 were waited for; matrix products, arithmetic and copies ran while one was open for 17% of the time, Pallas kernels for 0%

profile of v1, /device:TPU:2, one launch (start us, length us, event | category | flops | bytes accessed | tf_op | source)
XLA Modules:
  0.0 241.6 jit_solution(7706314357257257569)
XLA Ops:
  0.7 6.3 %copy.44 = bf16[2880,640]{0,1:T(8,128)(2,1)} copy(bf16[2880,640]{1,0:T(8,128)(2,1)} %param.15) | data formatting | bytes 7372800 | tf_op args[3]
  7.0 0.2 fusion.4
  7.2 0.8 fusion.6.rows_ref
  8.0 14.9 %gather_rows.1 = bf16[8,32,2880]{2,1,0:T(8,128)(2,1)} custom-call(bf16[32,2880]{1,0:T(8,128)(2,1)} %fusion.6.rows_ref), custom_call_target="tpu_custom_call" | custom-call | tf_op jit(solution)/shard_map/gather_rows/pallas_call | solution.py:214
  22.9 3.7 %convolution_bitcast_fusion = f32[256,1,10,64]{0,3,2,1:T(8,128)S(1)} fusion(bf16[256,2880,1]{1,0,2:T(8,128)(2,1)} %bitcast.126, bf16[10,64,2880]{2,1,0:T(8,128)(2,1)} %bitcast.125), kind=kOutput, calls=%fused_computation.6 | convolution fusion | flops 943718400 | bytes 5816320 | tf_op jit(solution)/shard_map/dot_general | solution.py:715
  26.7 0.8 copy-done.4
  27.5 0.2 reduce-window.8
  27.7 0.1 convert_reduce_fusion.2
  27.8 0.1 pad_add_fusion.2
  27.9 0.1 select_reduce_fusion.1
  28.0 0.2 fusion.20
  28.2 0.6 pad_maximum_fusion.3
  28.8 3.8 %collective-permute-start = (bf16[128,1,128]{0,2,1:T(8,128)(2,1)}, bf16[128,1,128]{0,2,1:T(8,128)(2,1)}, u32[]{:S(2)}, u32[]{:S(2)}) collective-permute-start(bf16[128,1,128]{0,2,1:T(8,128)(2,1)} %pad_maximum_fusion.3), channel_id=1, source_target_pairs={{0,8},{8,16},{16,24},{24,32},{32,40},{40,48},{48,56},{56,64},{64,7... | collective-permute-start | bytes 98312 | tf_op jit(solution)/shard_map/ppermute | solution.py:28
  32.6 0.6 copy_bitcast_fusion.1
  33.2 0.8 slice.119
  34.1 0.6 broadcast_compare_fusion.1
  34.7 0.6 add_add_fusion.1
  35.3 0.8 multiply_cosine_fusion
  36.1 0.7 copy.55
  36.8 0.7 copy.56
  37.5 0.1 reshape.1200
  37.6 0.1 reshape.1205
  37.7 0.1 convert_reduce_fusion.1
  37.8 0.7 copy.57
  38.5 0.4 convert_reduce_fusion
  39.0 0.1 select_reduce_fusion
  39.1 0.6 fusion.39
  39.7 0.1 fusion.26
  39.8 0.6 fusion.40
  40.4 0.5 broadcast_compare_fusion
  40.9 0.6 pad_add_fusion
  41.5 1.1 multiply_subtract_fusion
  42.7 1.6 maximum_bitcast_fusion
  44.3 0.8 fusion.38.home_ref
  45.1 1.6 fusion.13
  46.7 1.2 pad_clamp_fusion
  47.9 1.4 concatenate.80
  49.3 1.4 reduce_sum.90
  50.7 1.4 copy.48
  52.1 0.8 concatenate.85
  52.9 1.7 copy.50
  54.6 0.1 concatenate.86
  54.7 0.8 copy.51
  55.5 1.2 exp.27
  56.7 1.3 reshape.1198.gain_ref
  58.0 11.8 %copy.58 = bf16[1,2880,1440]{2,1,0:T(8,128)(2,1)} copy(bf16[1,2880,1440]{1,2,0:T(8,128)(2,1)} %param.21) | data formatting | bytes 16588800 | tf_op args[9]
  69.8 1.4 copy.59.routes_ref
  71.2 1.4 copy.60.gates_ref
  73.2 2.2 gather_fusion
  75.3 0.8 copy_bitcast_fusion
  76.1 0.8 maximum_maximum_fusion
  76.9 1.4 fusion
  78.4 0.5 fusion.1
  78.9 0.3 copy.53
  79.2 2.1 convolution_convert_fusion
  81.3 2.6 %copy.54 = bf16[256,2880]{1,0:T(8,128)(2,1)} copy(bf16[256,2880]{0,1:T(8,128)(2,1)} %convolution_convert_fusion) | data formatting | bytes 2949120 | tf_op jit(solution)/shard_map/convert_element_type | solution.py:741
  83.8 16.6 %sum_over_heads.1.sum_ref = f32[32,2880]{1,0:T(8,128)} custom-call(bf16[8,32,2880]{2,1,0:T(8,128)(2,1)} %bitcast.122), custom_call_target="tpu_custom_call" | custom-call | tf_op jit(solution)/shard_map/sum_over_heads/pallas_call | solution.py:279
  100.5 0.6 broadcast_in_dim.39.live_ref
  101.1 3.9 %prepare_chunks.1 = (f32[32,2880]{1,0:T(8,128)}, bf16[768,720]{1,0:T(8,128)(2,1)}) custom-call(f32[32,2880]{1,0:T(8,128)} %sum_over_heads.1.sum_ref, bf16[32,2880]{1,0:T(8,128)(2,1)} %tok_ref.1, f32[1,2880]{1,0:T(1,128)} %reshape.1198.gain_ref, s32[4,32]{1,0:T(4,128)} %bitcast.134, f32[1,128]{1,0:T(1,128)} %broadcast_in_dim.39.live_ref), custom_call_target="tpu_custom_call" | custom-call | tf_op jit(solution)/shard_map/prepare_chunks/pallas_call | solution.py:339
  105.0 52.5 %dispatch.1 = (bf16[2,64,24,720]{3,2,1,0:T(8,128)(2,1)}, bf16[16,16,128]{2,1,0:T(8,128)(2,1)}) custom-call(bf16[32,24,720]{2,1,0:T(8,128)(2,1)} %bitcast.127, bf16[16,16,128]{2,1,0:T(8,128)(2,1)} %gather_fusion), custom_call_target="tpu_custom_call" | custom-call | tf_op jit(solution)/shard_map/dispatch/pallas_call | solution.py:429
  157.5 25.1 %run_experts.1 = bf16[8,384,720]{2,1,0:T(8,128)(2,1)} custom-call(bf16[8,384,720]{2,1,0:T(8,128)(2,1)} %bitcast.123, bf16[2880,1440]{1,0:T(8,128)(2,1)} %bitcast.119, bf16[720,2880]{1,0:T(8,128)(2,1)} %bitcast.124), custom_call_target="tpu_custom_call" | custom-call | tf_op jit(solution)/shard_map/run_experts/pallas_call | solution.py:533
  182.7 54.4 %give_back.1 = bf16[64,24,720]{2,1,0:T(8,128)(2,1)} custom-call(bf16[2,64,24,720]{3,2,1,0:T(8,128)(2,1)} %bitcast.120), custom_call_target="tpu_custom_call" | custom-call | tf_op jit(solution)/shard_map/give_back/pallas_call | solution.py:617
  237.1 1.0 scatter_fusion
  238.1 3.4 %combine.1 = bf16[32,2880]{1,0:T(8,128)(2,1)} custom-call(bf16[1536,720]{1,0:T(8,128)(2,1)} %bitcast.121, f32[32,2880]{1,0:T(8,128)} %get-tuple-element.8.resid_ref, s32[32,4]{1,0:T(8,128)} %copy.59.routes_ref, f32[32,4]{1,0:T(8,128)} %copy.60.gates_ref, f32[1,128]{1,0:T(1,128)} %broadcast_in_dim.39.live_ref, s32[1,1536]{1,0:T(1,128)} %fusion.38.home_ref), custom_call_target="tpu_custom_call" | custom-call | tf_op jit(solution)/shard_map/combine/pallas_call | solution.py:674
  (46 shorter events, 0.3 us)
Async XLA Ops:
  0.6 78.6 %copy-start = (bf16[512,2880]{0,1:T(8,128)(2,1)S(1)}, bf16[512,2880]{0,1:T(8,128)(2,1)}, u32[]{:S(2)}) copy-start(bf16[512,2880]{0,1:T(8,128)(2,1)} %param.17) | copy-start | bytes 8847364
  0.7 6.3 %copy-start.1 = (bf16[32,2880]{1,0:T(8,128)(2,1)S(1)}, bf16[32,2880]{1,0:T(8,128)(2,1)}, u32[]{:S(2)}) copy-start(bf16[32,2880]{1,0:T(8,128)(2,1)} %tok_ref.1) | copy-start | bytes 552964
  0.7 6.5 %copy-start.9 = (f32[2880]{0:T(1024)S(1)}, f32[2880]{0:T(1024)}, u32[]{:S(2)}) copy-start(f32[2880]{0:T(1024)} %param.14) | copy-start | bytes 34564
  22.9 4.6 %copy-start.14 = (s32[4]{0:T(128)S(1)}, s32[4]{0:T(128)}, u32[]{:S(2)}) copy-start(s32[4]{0:T(128)} %param.13) | copy-start | bytes 52
  22.9 14.6 %copy-start.11 = (s32[256]{0:T(256)S(1)}, s32[256]{0:T(256)}, u32[]{:S(2)}) copy-start(s32[256]{0:T(256)} %param.23) | copy-start | bytes 3076
  26.7 0.8 copy-start.4
  27.8 13.7 %copy-start.10 = (s32[256]{0:T(256)}, s32[256]{0:T(256)S(1)}, u32[]{:S(2)}) copy-start(s32[256]{0:T(256)S(1)} %convert_reduce_fusion.2) | copy-start | bytes 3076
  28.8 46.5 %collective-permute-start = (bf16[128,1,128]{0,2,1:T(8,128)(2,1)}, bf16[128,1,128]{0,2,1:T(8,128)(2,1)}, u32[]{:S(2)}, u32[]{:S(2)}) collective-permute-start(bf16[128,1,128]{0,2,1:T(8,128)(2,1)} %pad_maximum_fusion.3), channel_id=1, source_target_pairs={{0,8},{8,16},{16,24},{24,32},{32,40},{40,48},{48,56},{56,64},{64,7... | collective-permute-start | bytes 98312 | tf_op jit(solution)/shard_map/ppermute | solution.py:28
  34.1 7.5 %copy-start.5 = (bf16[256,1,1,64]{0,3,2,1:T(8,128)(2,1)}, bf16[256,1,1,64]{0,3,2,1:T(8,128)(2,1)S(1)}, u32[]{:S(2)}) copy-start(bf16[256,1,1,64]{0,3,2,1:T(8,128)(2,1)S(1)} %slice.119) | copy-start | bytes 98308
  58.0 18.9 %copy-start.2 = (f32[2,128,8,32]{1,3,2,0:T(8,128)S(1)}, f32[2,128,8,32]{1,3,2,0:T(8,128)}, u32[]{:S(2)}) copy-start(f32[2,128,8,32]{1,3,2,0:T(8,128)} %copy.50) | copy-start | bytes 786436
  58.0 18.9 %copy-start.3 = (f32[2,128,8,32]{1,3,2,0:T(8,128)S(1)}, f32[2,128,8,32]{1,3,2,0:T(8,128)}, u32[]{:S(2)}) copy-start(f32[2,128,8,32]{1,3,2,0:T(8,128)} %copy.51) | copy-start | bytes 786436
  75.3 3.0 %copy-start.13 = (f32[8]{0:T(128)S(1)}, f32[8]{0:T(128)}, u32[]{:S(2)}) copy-start(f32[8]{0:T(128)} %exp.27) | copy-start | bytes 100
  75.3 3.1 %copy-start.6 = (pred[2,128,256]{1,2,0:T(8,128)(4,1)S(1)}, pred[2,128,256]{1,2,0:T(8,128)(4,1)}, u32[]{:S(2)}) copy-start(pred[2,128,256]{1,2,0:T(8,128)(4,1)} %fusion.13) | copy-start | bytes 196612
  182.6 54.5 %copy-start.8 = (bf16[16,16,128]{2,1,0:T(8,128)(2,1)S(1)}, bf16[16,16,128]{2,1,0:T(8,128)(2,1)}, u32[]{:S(2)}) copy-start(bf16[16,16,128]{2,1,0:T(8,128)(2,1)} %get-tuple-element.9) | copy-start | bytes 196612
  182.6 54.5 %copy-start.12 = (s32[16]{0:T(128)S(1)}, s32[16]{0:T(128)}, u32[]{:S(2)}) copy-start(s32[16]{0:T(128)} %fusion.40) | copy-start | bytes 196
  238.1 3.5 %copy-start.7 = (bf16[16,16,128]{2,1,0:T(8,128)(2,1)}, bf16[16,16,128]{2,1,0:T(8,128)(2,1)S(1)}, u32[]{:S(2)}) copy-start(bf16[16,16,128]{2,1,0:T(8,128)(2,1)S(1)} %scatter_fusion) | copy-start | bytes 196612

commit v2 on v0

v2 whole, which is shorter than its diff:
```python
import math

import jax
import jax.numpy as jnp
import numpy as np
from jax import lax
from jax.experimental import pallas as pl
from jax.experimental.pallas import tpu as pltpu
from jax.sharding import PartitionSpec as P

MODEL_WIDTH = 2880
HEAD_SIZE = 64
EXPERTS = 32
ATTEND_WINDOW = 128
PAGE_TOKENS = 16
QUERY_PER_KEY = 8

EPSILON = 1e-05
ROPE_BASE = 150000.0
GLU_ALPHA = 1.702

MESH = pl.DeviceIdType.MESH
VM = pltpu.VMEM
CHIPS = 64
ROWS = 32
SLOTS = 6
PARTS = 4
PART_WIDTH = MODEL_WIDTH // PARTS
CHUNK = PARTS * SLOTS
HEADS = 8


def vmem_spec():
    return pl.BlockSpec(memory_space=pltpu.VMEM)


def any_spec():
    return pl.BlockSpec(memory_space=pl.ANY)


def place():
    tok = lax.axis_index("tok")
    head = lax.axis_index("head")
    return (tok // 4, head // 2, tok % 4, head % 2)


def device(x, y, z, core):
    return (x * 4 + z, y * 2 + core)


def shifted(k, sign):
    x, y, z, core = place()
    dx, dy, dz = k // 16, (k // 4) % 4, k % 4
    if sign < 0:
        dx, dy, dz = 4 - dx, 4 - dy, 4 - dz
    return ((x + dx) % 4, (y + dy) % 4, (z + dz) % 4, core)


def sibling():
    x, y, z, core = place()
    return device(x, y, z, 1 - core)


def signal(barrier, target):
    pl.semaphore_signal(barrier, inc=1, device_id=target, device_id_type=MESH)

def far_first():
    def steps(k):
        return sum(min(d, 4 - d) for d in (k // 16, (k // 4) % 4, k % 4))

    return sorted(range(CHIPS), key=lambda k: -steps(k))


ORDER = far_first()


def greet_all(barrier):
    def greet(k, carry):
        signal(barrier, device(*shifted(k, 1)))
        return carry

    lax.fori_loop(1, CHIPS, greet, 0)
    signal(barrier, sibling())


def remote(src, dst, send, recv, target):
    return pltpu.make_async_remote_copy(
        src_ref=src, dst_ref=dst, send_sem=send, recv_sem=recv, device_id=target, device_id_type=MESH
    )


def iota(shape, dim):
    return lax.broadcasted_iota(jnp.int32, shape, dim)


def split_index(index, size):
    whole = jnp.floor((index.astype(jnp.float32) + 0.5) * (1.0 / size)).astype(jnp.int32)
    return (whole, index - whole * size)


TOK_ROWS = HEADS * ROWS
QKV = (QUERY_PER_KEY + 2) * HEAD_SIZE
LANES = 2 * HEAD_SIZE
HEAD_COLS = QUERY_PER_KEY * HEAD_SIZE
TOKS = 16


def swap_halves(values, lane):
    half = HEAD_SIZE // 2
    ahead = pltpu.roll(values, LANES - half, 1)
    behind = pltpu.roll(values, half, 1)
    return jnp.where(lane < half, ahead, behind)


def sequence_start(index, len_ref):
    start = jnp.zeros_like(index)
    end = jnp.int32(0)
    for s in range(4):
        end = end + len_ref[s]
        start = start + jnp.where(index >= end, len_ref[s], 0)
    return start, end


def expert_code(routes_ref, live):
    expert = iota((EXPERTS, ROWS), 0)
    routed = jnp.zeros((EXPERTS, ROWS), jnp.float32)
    for k in range(4):
        routed = routed + jnp.where(routes_ref[k : k + 1, :] == expert, 1.0, 0.0)
    routed = routed * live
    earlier = jnp.where(iota((ROWS, ROWS), 0) < iota((ROWS, ROWS), 1), 1.0, 0.0)
    rank = jnp.dot(
        routed.astype(jnp.bfloat16), earlier.astype(jnp.bfloat16), preferred_element_type=jnp.float32
    )
    return jnp.where(routed > 0.5, rank, -1.0).astype(jnp.bfloat16)


def block_live(len_ref, tok, head):
    total = len_ref[0] + len_ref[1] + len_ref[2] + len_ref[3]
    index = iota((EXPERTS, ROWS), 1) + (tok * TOK_ROWS + head * ROWS)
    return jnp.where(index < total, 1.0, 0.0)


def front_kernel(
    tok_ref,
    gain_attn_ref,
    gain_moe_ref,
    len_ref,
    routes_ref,
    table_ref,
    sinks_ref,
    wqkv_ref,
    wout_ref,
    resid_ref,
    recv_ref,
    arrived_ref,
    xn,
    wq,
    wo,
    halo,
    kvs,
    att,
    part,
    pair,
    sums,
    far,
    outg,
    pages,
    wsem,
    asend,
    arecv,
    fsend,
    frecv,
    hsem,
    psend,
    precv,
    rsend,
    rrecv,
    gsend,
    grecv,
    csend,
    crecv,
    bsend,
    brecv,
    local,
):
    x, y, z, core = place()
    tok = x * 4 + z
    head = y * 2 + core
    sib = sibling()
    barrier = pltpu.get_barrier_semaphore()
    greet_all(barrier)
    load_q = pltpu.make_async_copy(wqkv_ref, wq, wsem.at[0])
    load_o = pltpu.make_async_copy(wout_ref, wo, wsem.at[1])
    load_q.start()
    load_o.start()

    mine = y * 2 + core
    lower = ((y + 3) % 4) * 2 + core
    upper = ((y + 1) % 4) * 2 + core
    opposite = ((y + 2) % 4) * 2 + core
    wide = tok_ref[...].astype(jnp.float32)
    inv_rms = lax.rsqrt(jnp.mean(wide * wide, axis=-1, keepdims=True) + EPSILON)
    xn[mine] = (wide * inv_rms * gain_attn_ref[...]).astype(jnp.bfloat16)
    pl.semaphore_wait(barrier, CHIPS)

    up = device(x, (y + 1) % 4, z, core)
    down = device(x, (y + 3) % 4, z, core)
    half = ROWS // 2
    first = pl.ds(0, half)
    second = pl.ds(half, half)
    to_up = remote(xn.at[mine], xn.at[mine], asend.at[0], arecv.at[0], up)
    to_down = remote(xn.at[mine], xn.at[mine], asend.at[1], arecv.at[1], down)
    to_sib = remote(xn.at[mine], xn.at[mine], fsend.at[0], frecv.at[0], sib)
    to_up.start()
    to_down.start()
    to_sib.start()

    lane = iota((TOK_ROWS, LANES), 1)
    lane64 = jnp.where(lane < HEAD_SIZE, lane, lane - HEAD_SIZE)
    lane32 = jnp.where(lane64 < HEAD_SIZE // 2, lane64, lane64 - HEAD_SIZE // 2)
    index = iota((TOK_ROWS, LANES), 0) + tok * TOK_ROWS
    start, total = sequence_start(index, len_ref)
    rate = jnp.exp(lane32.astype(jnp.float32) * (-2.0 * math.log(ROPE_BASE) / HEAD_SIZE))
    angle = (index - start).astype(jnp.float32) * rate
    cos_table = jnp.cos(angle)
    sin_table = jnp.where(lane64 < HEAD_SIZE // 2, -jnp.sin(angle), jnp.sin(angle))

    to_up.wait_recv()
    on_up = remote(xn.at[lower, first], xn.at[lower, first], asend.at[2], arecv.at[2], up)
    on_up.start()
    sib_low = remote(xn.at[lower], xn.at[lower], fsend.at[1], frecv.at[1], sib)
    sib_low.start()
    to_down.wait_recv()
    on_down = remote(xn.at[upper, second], xn.at[upper, second], asend.at[3], arecv.at[3], down)
    on_down.start()
    sib_up = remote(xn.at[upper], xn.at[upper], fsend.at[2], frecv.at[2], sib)
    sib_up.start()
    on_up.wait_recv()
    on_down.wait_recv()
    sib_far = remote(xn.at[opposite], xn.at[opposite], fsend.at[3], frecv.at[3], sib)
    sib_far.start()
    for copy in (to_sib, sib_low, sib_up, sib_far):
        copy.wait_recv()
    load_q.wait()

    projected = jnp.dot(
        xn[...].reshape(TOK_ROWS, MODEL_WIDTH), wq[...], preferred_element_type=jnp.float32
    )

    slab = projected[:, HEAD_COLS:]
    turned = slab * cos_table + swap_halves(slab, lane64) * sin_table
    kvs[...] = jnp.where(lane < HEAD_SIZE, turned, slab).astype(jnp.bfloat16)
    after = (tok + 1) % TOKS
    to_next = remote(
        kvs.at[pl.ds(TOK_ROWS - ATTEND_WINDOW, ATTEND_WINDOW)],
        halo,
        hsem.at[0],
        hsem.at[1],
        (after, head),
    )
    to_next.start()
    queries = []
    for s in range(HEAD_COLS // LANES):
        slab = projected[:, s * LANES : (s + 1) * LANES]
        turned = slab * cos_table + swap_halves(slab, lane64) * sin_table
        queries.append(turned * HEAD_SIZE ** (-0.5))

    row_page, row_in = split_index(iota((TOK_ROWS, TOK_ROWS), 0), PAGE_TOKENS)
    col_page, col_in = split_index(iota((TOK_ROWS, TOK_ROWS), 1), PAGE_TOKENS)
    col_of = split_index(iota((1, TOK_ROWS), 1), PAGE_TOKENS)[0]
    target = jnp.zeros((1, TOK_ROWS), jnp.int32)
    for p in range(TOKS):
        target = target + jnp.where(col_of == p, table_ref[tok * TOKS + p] // TOKS, 0)
    pick = jnp.where((target == row_page) & (row_in == col_in), 1.0, 0.0).astype(jnp.bfloat16)
    sorted_rows = jnp.dot(pick, kvs[...], preferred_element_type=jnp.float32).astype(jnp.bfloat16)
    pages[...] = sorted_rows.reshape(TOKS, PAGE_TOKENS, LANES)

    def page(j):
        tx, tz = (x + j // 4) % 4, (z + j % 4) % 4
        return remote(
            pages.at[tx * 4 + tz], arrived_ref.at[tok], gsend.at[j], grecv.at[j], device(tx, y, tz, core)
        )

    def attend(b):
        wide_halo = halo[...].astype(jnp.float32)
        wide_kv = kvs[...].astype(jnp.float32)
        if b == 0:
            before = jnp.where(tok * jnp.ones_like(wide_halo) > 0.5, wide_halo, 0.0)
            band = jnp.concatenate([before, wide_kv[:ATTEND_WINDOW]], axis=0)
        else:
            band = wide_kv
        turned = pltpu.roll(band, HEAD_SIZE, 1)
        lanes = iota((2 * ATTEND_WINDOW, LANES), 1)
        keys = jnp.where(lanes < HEAD_SIZE, band, turned).astype(jnp.bfloat16)
        values = jnp.where(lanes < HEAD_SIZE, turned, band).astype(jnp.bfloat16)
        lo = iota((ATTEND_WINDOW, LANES), 1) < HEAD_SIZE
        stack = []
        for s in range(HEAD_COLS // LANES):
            rows = queries[s][b * ATTEND_WINDOW : (b + 1) * ATTEND_WINDOW]
            stack.append(jnp.where(lo, rows, 0.0).astype(jnp.bfloat16))
            stack.append(jnp.where(lo, 0.0, rows).astype(jnp.bfloat16))
        scores = lax.dot_general(
            jnp.concatenate(stack, axis=0),
            keys,
            (((1,), (1,)), ((), ())),
            preferred_element_type=jnp.float32,
        )
        shape = (ATTEND_WINDOW, 2 * ATTEND_WINDOW)
        query = iota(shape, 0) + (tok * TOK_ROWS + b * ATTEND_WINDOW)
        began, ends = sequence_start(query, len_ref)
        distance = iota(shape, 0) + ATTEND_WINDOW - iota(shape, 1)
        reach = jnp.minimum(query - began, ATTEND_WINDOW - 1)
        allowed = (distance >= 0) & (distance <= reach) & (query < ends)
        sink = jnp.exp(sinks_ref[...])
        probs = []
        for n in range(QUERY_PER_KEY):
            block = scores[n * ATTEND_WINDOW : (n + 1) * ATTEND_WINDOW]
            weights = jnp.where(allowed, jnp.exp(block), 0.0)
            totals = jnp.sum(weights, axis=-1, keepdims=True) + sink[0:1, n : n + 1]
            probs.append((weights / totals).astype(jnp.bfloat16))
        mixed = jnp.dot(
            jnp.concatenate(probs, axis=0), values, preferred_element_type=jnp.float32
        )
        for s in range(HEAD_COLS // LANES):
            even = mixed[2 * s * ATTEND_WINDOW : (2 * s + 1) * ATTEND_WINDOW]
            odd = mixed[(2 * s + 1) * ATTEND_WINDOW : (2 * s + 2) * ATTEND_WINDOW]
            both = jnp.where(lo, even, odd).astype(jnp.bfloat16)
            att[b * 4 : (b + 1) * 4, :, s * LANES : (s + 1) * LANES] = both.reshape(4, ROWS, LANES)

    def start_page(j, carry):
        page(j).start()
        return carry

    own_page = pltpu.make_async_copy(pages.at[tok], arrived_ref.at[tok], local.at[1])
    attend(1)
    lax.fori_loop(1, TOKS, start_page, 0)
    own_page.start()
    to_next.wait_recv()
    attend(0)
    load_o.wait()

    owners = [(y + 1) % 4, (y + 2) % 4, (y + 3) % 4, y]
    contract = (((1,), (1,)), ((), ()))
    rows = jnp.concatenate([att[o * 2 + 1 - core] for o in owners], axis=0)
    theirs = lax.dot_general(rows, wo[...], contract, preferred_element_type=jnp.float32)
    part[...] = theirs.astype(jnp.bfloat16).reshape(4, ROWS, MODEL_WIDTH)
    pairs = []
    for i in range(4):
        copy = remote(part.at[i], pair.at[i], psend.at[i], precv.at[i], sib)
        copy.start()
        pairs.append(copy)
    rows = jnp.concatenate([att[o * 2 + core] for o in owners], axis=0)
    ours = lax.dot_general(rows, wo[...], contract, preferred_element_type=jnp.float32)
    sent = []
    for i in range(4):
        pairs[i].wait_recv()
        both = ours[i * ROWS : (i + 1) * ROWS] + pair[i].astype(jnp.float32)
        if i < 3:
            sums[i] = both.astype(jnp.bfloat16)
        if i > 0:
            copy = remote(
                sums.at[i - 1], far.at[i - 1], rsend.at[i - 1], rrecv.at[i - 1], device(x, owners[i - 1], z, core)
            )
            copy.start()
            sent.append(copy)

    code = expert_code(routes_ref, block_live(len_ref, tok, head))
    count = EXPERTS * CHUNK
    owner, _ = split_index(iota((count, EXPERTS), 0), CHUNK)
    spread = jnp.where(owner == iota((count, EXPERTS), 1), 1.0, 0.0).astype(jnp.bfloat16)
    code_rows = jnp.dot(spread, code, preferred_element_type=jnp.float32)
    _, within = split_index(iota((count, ROWS), 0), CHUNK)
    quarter, slot = split_index(within, SLOTS)
    hit = jnp.abs(code_rows - slot.astype(jnp.float32)) < 0.5
    picks = [
        jnp.where(hit & (quarter == q), 1.0, 0.0).astype(jnp.bfloat16) for q in range(PARTS)
    ]

    resid = tok_ref[...].astype(jnp.float32) + both
    for i in range(3):
        sent[i].wait_recv()
        resid = resid + far[i].astype(jnp.float32)
    resid_ref[...] = resid
    inv_rms = lax.rsqrt(jnp.mean(resid * resid, axis=-1, keepdims=True) + EPSILON)
    moe_in = (resid * inv_rms * gain_moe_ref[...]).astype(jnp.bfloat16)
    chunks = jnp.zeros((count, PART_WIDTH), jnp.float32)
    for q in range(PARTS):
        chunks = chunks + jnp.dot(
            picks[q],
            moe_in[:, q * PART_WIDTH : (q + 1) * PART_WIDTH],
            preferred_element_type=jnp.float32,
        )
    outg[...] = chunks.reshape(EXPERTS, CHUNK, PART_WIDTH).astype(jnp.bfloat16)

    for i in range(CHIPS - 1):
        tx, ty, tz, tc = shifted(ORDER[i], 1)
        expert = (tx * 4 + tz) * 2 + ty // 2
        remote(
            outg.at[expert], recv_ref.at[0, i], csend.at[i], crecv.at[i], device(tx, ty, tz, tc)
        ).start()
    own = pltpu.make_async_copy(outg.at[tok * 2 + y // 2], recv_ref.at[0, CHIPS - 1], local.at[0])
    own.start()

    def received(i):
        return remote(outg.at[0], recv_ref.at[0, i], csend.at[i], crecv.at[i], sib)

    def forward(g):
        block = pl.ds(g * 8, 8)
        return remote(recv_ref.at[0, block], recv_ref.at[1, block], bsend.at[g], brecv.at[g], sib)

    def arrive(i, carry):
        received(i).wait_recv()
        return carry

    def pass_on(g, carry):
        lax.fori_loop(g * 8, g * 8 + 8, arrive, 0)
        forward(g).start()
        return carry

    lax.fori_loop(0, 7, pass_on, 0)
    own.wait()
    lax.fori_loop(CHIPS - 8, CHIPS - 1, arrive, 0)
    forward(7).start()

    def finish_forward(g, carry):
        forward(g).wait()
        return carry

    def finish_chunk(i, carry):
        received(i).wait_send()
        return carry

    def finish_page(j, carry):
        page(j).wait()
        return carry

    lax.fori_loop(0, 8, finish_forward, 0)
    lax.fori_loop(0, CHIPS - 1, finish_chunk, 0)
    lax.fori_loop(1, TOKS, finish_page, 0)
    own_page.wait()
    for copy in pairs + sent + [to_up, to_down, on_up, on_down, to_sib, sib_low, sib_up, sib_far]:
        copy.wait_send()
    to_next.wait_send()


def front(tokens, gain_attn, gain_moe, lengths, routes_t, page_table, sinks, w_qkv, w_out_t):
    bf, dma = jnp.bfloat16, pltpu.SemaphoreType.DMA
    smem = pl.BlockSpec(memory_space=pltpu.SMEM)
    return pl.pallas_call(
        front_kernel,
        out_shape=(
            jax.ShapeDtypeStruct((ROWS, MODEL_WIDTH), jnp.float32),
            jax.ShapeDtypeStruct((2, CHIPS, CHUNK, PART_WIDTH), bf),
            jax.ShapeDtypeStruct((TOKS, PAGE_TOKENS, LANES), bf),
        ),
        in_specs=[
            vmem_spec(),
            vmem_spec(),
            vmem_spec(),
            smem,
            vmem_spec(),
            smem,
            vmem_spec(),
            any_spec(),
            any_spec(),
        ],
        out_specs=(vmem_spec(), any_spec(), any_spec()),
        scratch_shapes=[
            VM((HEADS, ROWS, MODEL_WIDTH), bf),
            VM((MODEL_WIDTH, QKV), bf),
            VM((MODEL_WIDTH, HEAD_COLS), bf),
            VM((ATTEND_WINDOW, LANES), bf),
            VM((TOK_ROWS, LANES), bf),
            VM((HEADS, ROWS, HEAD_COLS), bf),
            VM((4, ROWS, MODEL_WIDTH), bf),
            VM((4, ROWS, MODEL_WIDTH), bf),
            VM((3, ROWS, MODEL_WIDTH), bf),
            VM((3, ROWS, MODEL_WIDTH), bf),
            VM((EXPERTS, CHUNK, PART_WIDTH), bf),
            VM((TOKS, PAGE_TOKENS, LANES), bf),
            dma((2,)),
            dma((4,)),
            dma((4,)),
            dma((4,)),
            dma((4,)),
            dma((2,)),
            dma((4,)),
            dma((4,)),
            dma((3,)),
            dma((3,)),
            dma((TOKS,)),
            dma((TOKS,)),
            dma((CHIPS,)),
            dma((CHIPS,)),
            dma((8,)),
            dma((8,)),
            dma((2,)),
        ],
        compiler_params=pltpu.CompilerParams(
            collective_id=0, has_side_effects=True, vmem_limit_bytes=60 << 20
        ),
        name="front",
    )(
        tokens,
        gain_attn.reshape(1, MODEL_WIDTH),
        gain_moe.reshape(1, MODEL_WIDTH),
        lengths,
        routes_t,
        page_table,
        sinks.reshape(1, QUERY_PER_KEY),
        w_qkv,
        w_out_t,
    )


GROUPS = 8
GROUP_ROWS = 2 * CHIPS * CHUNK // GROUPS
GROUP_SLOTS = GROUP_ROWS // PARTS
EXPERT_ROWS = GROUPS * GROUP_SLOTS
DOT_ROWS = 256


def sorting(transposed):
    shape = (GROUP_ROWS, GROUP_ROWS)
    dim = 1 if transposed else 0
    quarter, row = split_index(iota(shape, dim), GROUP_SLOTS)
    row_source, row_slot = split_index(row, SLOTS)
    col_source, col = split_index(iota(shape, 1 - dim), CHUNK)
    col_quarter, col_slot = split_index(col, SLOTS)
    match = (quarter == col_quarter) & (row_source == col_source) & (row_slot == col_slot)
    return jnp.where(match, 1.0, 0.0).astype(jnp.bfloat16)


def place_pages(arrived_ref, table_ref, cache_ref):
    tok = lax.axis_index("tok")
    page, slot = split_index(table_ref[...], TOKS)
    landing = jnp.sum(jnp.where(page == tok, slot, 0).astype(jnp.float32), axis=0, keepdims=True)
    col_page, _ = split_index(iota((TOKS, TOK_ROWS), 1), PAGE_TOKENS)
    widen = jnp.where(col_page == iota((TOKS, TOK_ROWS), 0), 1.0, 0.0).astype(jnp.bfloat16)
    lands = jnp.dot(landing.astype(jnp.bfloat16), widen, preferred_element_type=jnp.float32)
    row_page, row_in = split_index(iota((TOK_ROWS, TOK_ROWS), 0), PAGE_TOKENS)
    _, col_in = split_index(iota((TOK_ROWS, TOK_ROWS), 1), PAGE_TOKENS)
    hit = (jnp.abs(lands - row_page.astype(jnp.float32)) < 0.5) & (row_in == col_in)
    pick = jnp.where(hit, 1.0, 0.0).astype(jnp.bfloat16)
    cache_ref[...] = jnp.dot(pick, arrived_ref[...], preferred_element_type=jnp.float32).astype(
        jnp.bfloat16
    )


def expert_kernel(
    recv_ref, win_ref, wdown_ref, arrived_ref, table_ref, y_ref, cache_ref, rbuf, w1, w2, xs, acts, ys, sem
):
    copies_r = [
        pltpu.make_async_copy(recv_ref.at[b], rbuf.at[b], sem.at[b]) for b in range(GROUPS)
    ]
    copy_w = pltpu.make_async_copy(win_ref, w1, sem.at[GROUPS])
    copy_d = pltpu.make_async_copy(wdown_ref, w2, sem.at[GROUPS + 1])
    for copy in copies_r + [copy_w, copy_d]:
        copy.start()
    place_pages(arrived_ref, table_ref, cache_ref)
    perm = sorting(False)
    back = sorting(True)
    for copy in copies_r:
        copy.wait()

    def sort_in(b, carry):
        mixed = jnp.dot(perm, rbuf[b], preferred_element_type=jnp.float32).astype(jnp.bfloat16)
        rows = pl.ds(pl.multiple_of(b * GROUP_SLOTS, GROUP_SLOTS), GROUP_SLOTS)
        for q in range(PARTS):
            xs[rows, q * PART_WIDTH : (q + 1) * PART_WIDTH] = mixed[
                q * GROUP_SLOTS : (q + 1) * GROUP_SLOTS
            ]
        return carry

    lax.fori_loop(0, GROUPS, sort_in, 0)
    copy_w.wait()
    contract = (((1,), (1,)), ((), ()))

    def up_block(i, carry):
        rows = pl.ds(pl.multiple_of(i * DOT_ROWS, DOT_ROWS), DOT_ROWS)
        here = xs[rows, :]
        gate = lax.dot_general(
            here, w1[:PART_WIDTH, :], contract, preferred_element_type=jnp.float32
        )
        up = lax.dot_general(
            here, w1[PART_WIDTH:, :], contract, preferred_element_type=jnp.float32
        )
        act = (up + 1.0) * gate * jax.nn.sigmoid(GLU_ALPHA * gate)
        acts[rows, :] = act.astype(jnp.bfloat16)
        return carry

    lax.fori_loop(0, EXPERT_ROWS // DOT_ROWS, up_block, 0)
    copy_d.wait()

    def down_block(i, carry):
        rows = pl.ds(pl.multiple_of(i * DOT_ROWS, DOT_ROWS), DOT_ROWS)
        down = jnp.dot(acts[rows, :], w2[...], preferred_element_type=jnp.float32)
        down = down.astype(jnp.bfloat16)
        for q in range(PARTS):
            ys[q, rows, :] = down[:, q * PART_WIDTH : (q + 1) * PART_WIDTH]
        return carry

    lax.fori_loop(0, EXPERT_ROWS // DOT_ROWS, down_block, 0)

    def sort_out(b, carry):
        rows = pl.ds(pl.multiple_of(b * GROUP_SLOTS, GROUP_SLOTS), GROUP_SLOTS)
        stacked = jnp.concatenate([ys[q, rows, :] for q in range(PARTS)], axis=0)
        y_ref[b] = jnp.dot(back, stacked, preferred_element_type=jnp.float32).astype(jnp.bfloat16)
        return carry

    lax.fori_loop(0, GROUPS, sort_out, 0)


def run_experts(received, w_in_t, w_down, arrived, table_t):
    out, cache = pl.pallas_call(
        expert_kernel,
        out_shape=(
            jax.ShapeDtypeStruct((GROUPS, GROUP_ROWS, PART_WIDTH), jnp.bfloat16),
            jax.ShapeDtypeStruct((TOK_ROWS, LANES), jnp.bfloat16),
        ),
        in_specs=[any_spec()] * 3 + [vmem_spec()] * 2,
        out_specs=(vmem_spec(), vmem_spec()),
        scratch_shapes=[
            VM((GROUPS, GROUP_ROWS, PART_WIDTH), jnp.bfloat16),
            VM((2 * PART_WIDTH, MODEL_WIDTH), jnp.bfloat16),
            VM((PART_WIDTH, MODEL_WIDTH), jnp.bfloat16),
            VM((EXPERT_ROWS, MODEL_WIDTH), jnp.bfloat16),
            VM((EXPERT_ROWS, PART_WIDTH), jnp.bfloat16),
            VM((PARTS, EXPERT_ROWS, PART_WIDTH), jnp.bfloat16),
            pltpu.SemaphoreType.DMA((GROUPS + 2,)),
        ],
        compiler_params=pltpu.CompilerParams(vmem_limit_bytes=60 << 20),
        name="run_experts",
    )(
        received.reshape(GROUPS, GROUP_ROWS, PART_WIDTH),
        w_in_t,
        w_down,
        arrived.reshape(TOK_ROWS, LANES),
        table_t,
    )
    return (out.reshape(2, CHIPS, CHUNK, PART_WIDTH), cache)


def return_kernel(y_ref, ret_ref, own, pair, sums, psend, precv, send, recv, lsem, last):
    barrier = pltpu.get_barrier_semaphore()
    sib = sibling()
    greet_all(barrier)

    def load(g):
        block = pl.ds(g * 8, 8)
        return pltpu.make_async_copy(y_ref.at[0, block], own.at[block], lsem.at[g])

    def start_load(g, carry):
        load(g).start()
        return carry

    lax.fori_loop(0, 8, start_load, 0)
    pl.semaphore_wait(barrier, CHIPS)

    def exchange(g):
        block = pl.ds(g * 8, 8)
        return remote(y_ref.at[1, block], pair.at[block], psend.at[g], precv.at[g], sib)

    def start_exchange(g, carry):
        exchange(g).start()
        return carry

    lax.fori_loop(0, 8, start_exchange, 0)

    def start_group(g):
        for i in range(g * 8, min(g * 8 + 8, CHIPS - 1)):
            remote(
                sums.at[i], ret_ref.at[i], send.at[i], recv.at[i], device(*shifted(ORDER[i], -1))
            ).start()

    for g in range(8):
        exchange(g).wait_recv()
        load(g).wait()
        block = pl.ds(g * 8, 8)
        sums[block] = (own[block].astype(jnp.float32) + pair[block].astype(jnp.float32)).astype(
            jnp.bfloat16
        )
        if g > 0:
            start_group(g - 1)
    start_group(7)
    home = pltpu.make_async_copy(sums.at[CHIPS - 1], ret_ref.at[CHIPS - 1], last)
    home.start()

    def finish_exchange(g, carry):
        exchange(g).wait_send()
        return carry

    def finish_chunk(i, carry):
        remote(sums.at[i], ret_ref.at[i], send.at[i], recv.at[i], sib).wait()
        return carry

    lax.fori_loop(0, 8, finish_exchange, 0)
    lax.fori_loop(0, CHIPS - 1, finish_chunk, 0)
    home.wait()


def give_back(y):
    return pl.pallas_call(
        return_kernel,
        out_shape=jax.ShapeDtypeStruct((CHIPS, CHUNK, PART_WIDTH), jnp.bfloat16),
        in_specs=[any_spec()],
        out_specs=any_spec(),
        scratch_shapes=[
            VM((CHIPS, CHUNK, PART_WIDTH), jnp.bfloat16),
            VM((CHIPS, CHUNK, PART_WIDTH), jnp.bfloat16),
            VM((CHIPS, CHUNK, PART_WIDTH), jnp.bfloat16),
            pltpu.SemaphoreType.DMA((8,)),
            pltpu.SemaphoreType.DMA((8,)),
            pltpu.SemaphoreType.DMA((CHIPS,)),
            pltpu.SemaphoreType.DMA((CHIPS,)),
            pltpu.SemaphoreType.DMA((8,)),
            pltpu.SemaphoreType.DMA,
        ],
        compiler_params=pltpu.CompilerParams(collective_id=3, has_side_effects=True),
        name="give_back",
    )(y)


def combine_kernel(ret_ref, resid_ref, routes_ref, gates_ref, len_ref, shift_ref, out_ref):
    x, y, z, core = place()
    live = block_live(len_ref, x * 4 + z, y * 2 + core)
    expert = iota((EXPERTS, ROWS), 0)
    gate = jnp.zeros((EXPERTS, ROWS), jnp.float32)
    for k in range(4):
        gate = gate + jnp.where(routes_ref[k : k + 1, :] == expert, gates_ref[k : k + 1, :], 0.0)
    code = expert_code(routes_ref, live)
    count = CHIPS * CHUNK
    tx, rest = split_index(shift_ref[...], 16)
    ty, tz = split_index(rest, 4)

    def wrapped(value):
        return jnp.where(value >= 4, value - 4, value)

    half = jnp.where(wrapped(ty + y) >= 2, 1, 0)
    home = (wrapped(tx + x) * 4 + wrapped(tz + z)) * 2 + half
    spread = jnp.where(iota((EXPERTS, count), 0) == home, 1.0, 0.0).astype(jnp.bfloat16)
    contract = (((0,), (0,)), ((), ()))
    code_cols = lax.dot_general(code, spread, contract, preferred_element_type=jnp.float32)
    gate_cols = lax.dot_general(
        gate.astype(jnp.bfloat16), spread, contract, preferred_element_type=jnp.float32
    )
    _, within = split_index(iota((ROWS, count), 1), CHUNK)
    quarter, slot = split_index(within, SLOTS)
    weight = jnp.where(jnp.abs(code_cols - slot.astype(jnp.float32)) < 0.5, gate_cols, 0.0)
    stacked = jnp.concatenate(
        [jnp.where(quarter == q, weight, 0.0).astype(jnp.bfloat16) for q in range(PARTS)], axis=0
    )
    total = jnp.dot(stacked, ret_ref[...], preferred_element_type=jnp.float32)
    for q in range(PARTS):
        cols = slice(q * PART_WIDTH, (q + 1) * PART_WIDTH)
        out_ref[:, cols] = (resid_ref[:, cols] + total[q * ROWS : (q + 1) * ROWS]).astype(
            jnp.bfloat16
        )


def combine(returned, resid, routes_t, gates_t, lengths):
    shifts = jnp.asarray(np.repeat(np.array(ORDER, np.int32), CHUNK)[None, :])
    return pl.pallas_call(
        combine_kernel,
        out_shape=jax.ShapeDtypeStruct((ROWS, MODEL_WIDTH), jnp.bfloat16),
        in_specs=[vmem_spec()] * 4 + [pl.BlockSpec(memory_space=pltpu.SMEM), vmem_spec()],
        out_specs=vmem_spec(),
        name="combine",
    )(returned.reshape(CHIPS * CHUNK, PART_WIDTH), resid, routes_t, gates_t, lengths, shifts)


def per_device(
    tokens,
    lengths,
    norm_gain_attn,
    query_key_value_weight,
    sinks,
    w_out_attn,
    norm_gain_moe,
    routes,
    gates,
    w_in,
    w_down,
    page_table,
):
    routes_t = jnp.transpose(routes)
    resid, received, arrived = front(
        tokens,
        norm_gain_attn,
        norm_gain_moe,
        lengths,
        routes_t,
        page_table,
        sinks,
        query_key_value_weight,
        jnp.transpose(w_out_attn),
    )
    produced, cache = run_experts(
        received, jnp.transpose(w_in[0]), w_down[0], arrived, jnp.transpose(page_table.reshape(TOKS, TOKS))
    )
    hidden_out = combine(give_back(produced), resid, routes_t, jnp.transpose(gates), lengths)
    return (hidden_out, cache.reshape(1, TOKS, PAGE_TOKENS, LANES))


def solution(mesh):
    return jax.shard_map(
        per_device,
        mesh=mesh,
        in_specs=(
            P(("tok", "head"), None),
            P(),
            P(),
            P(None, "head"),
            P("head"),
            P("head", None),
            P(),
            P(("tok", "head"), None),
            P(("tok", "head"), None),
            P(("tok", "head"), None, None),
            P(("tok", "head"), None, None),
            P(),
        ),
        out_specs=(P(("tok", "head"), None), P("head", "tok", None, None)),
        check_vma=False,
    )
```

time: 339 us -> 154 us (0.45)
  waiting for transfers between devices: 196 us -> 0 us
  Pallas kernels: 0 us -> 149 us
  local copies, waits for them, and re-layouts: 50.4 us -> 4.06 us
  matrix products: 27.2 us -> 0 us
  starting transfers between devices: 25.7 us -> 0 us
  other arithmetic: 22.7 us -> 0 us
  between operations: 14.5 us -> 0.66 us
    pallas_call x0 -> x4, Pallas kernels: none -> 149 us  [the longest x1 75.2 us: front(): pl.pallas_call(front_kernel, out_shape=(jax.ShapeDtypeStruct((ROWS, MODEL...]
    all_to_all x3 -> x0, waiting for transfers between devices: 142 us -> none  [the longest x2 142 us: flat_route(): lax.all_to_all(blocks, ('tok', 'head'), split_axis=0, concat_axis=0, tile...]
    reduce_scatter x1 -> x0, waiting for transfers between devices: 32.2 us -> none  [per_device(): lax.psum_scatter(jnp.dot(attended, w_out_attn, preferred_element_type=jnp...]
    dot_general x6 -> x0, matrix products: 27.2 us -> none  [the longest x1 10.8 us: expert_mlp(): gate_up = jnp.dot(rows_in, w_in_local, preferred_element_type=jnp.float32)]
    all_gather x1 -> x0, waiting for transfers between devices: 22.3 us -> none  [per_device(): lax.all_gather(normed_input, 'head', axis=0, tiled=True)]
    all_to_all x3 -> x0, starting transfers between devices: 22.2 us -> none  [the longest x2 14.8 us: flat_route(): lax.all_to_all(blocks, ('tok', 'head'), split_axis=0, concat_axis=0, tile...]
    reshape x5 -> x4, local copies, waits for them, and re-layouts: 19 us -> 4.06 us  [the longest x2 1.43 us: per_device(): page_table.reshape(TOKS, TOKS)]
    reduce_sum x13 -> x0, other arithmetic: 11.9 us -> none  [the longest x1 5.95 us: copied_route(): jnp.sum(returned.astype(jnp.float32).reshape(EXPERTS, width_split, slots,...]
  transfers between devices with their start and end apart: 6 -> 0, of which waited for: 4 -> 0; matrix products, arithmetic and copies ran while one was open for 17% -> 0% of each run, Pallas kernels for 0% -> 0%
where the time goes in v2:
time: 154 us
  Pallas kernels  149 us (97%)
  local copies, waits for them, and re-layouts  4.06 us (3%)
    pallas_call x1, Pallas kernels, front(): pl.pallas_call(front_kernel, out_shape=(jax.ShapeDtypeStruct((ROWS, MODEL...  75.2 us
    pallas_call x1, Pallas kernels, give_back(): pl.pallas_call(return_kernel, out_shape=jax.ShapeDtypeStruct((CHIPS, CHUN...  44.2 us
    pallas_call x1, Pallas kernels, run_experts(): pl.pallas_call(expert_kernel, out_shape=(jax.ShapeDtypeStruct((GROUPS, GR...  26.2 us
    pallas_call x1, Pallas kernels, combine(): pl.pallas_call(combine_kernel, out_shape=jax.ShapeDtypeStruct((ROWS, MODE...  3.4 us

profile of v2, /device:TPU:2, one launch (start us, length us, event | category | flops | bytes accessed | tf_op | source)
XLA Modules:
  0.0 153.7 jit_solution(1973871512358044234)
XLA Ops:
  0.6 0.8 reshape.36
  1.4 0.7 copy.15
  2.1 1.3 reshape.31.gain_attn_ref
  3.4 1.3 reshape.32.gain_moe_ref
  4.7 75.2 %front.1 = (f32[32,2880]{1,0:T(8,128)}, bf16[2,64,24,720]{3,2,1,0:T(8,128)(2,1)}, bf16[16,16,128]{2,1,0:T(8,128)(2,1)}) custom-call(bf16[32,2880]{1,0:T(8,128)(2,1)} %tok_ref.1, f32[1,2880]{1,0:T(1,128)} %reshape.31.gain_attn_ref, f32[1,2880]{1,0:T(1,128)} %reshape.32.gain_moe_ref, s32[4]{0:T(128)} %len_ref.3, s32[4,32]{1,0:T(4,128)} %bitcast.22, ...), custom_call_target="tpu_custom_call" | custom-call | tf_op jit(solution)/shard_map/front/pallas_call | solution.py:449
  79.9 26.2 %run_experts.1 = (bf16[8,384,720]{2,1,0:T(8,128)(2,1)}, bf16[256,128]{1,0:T(8,128)(2,1)}) custom-call(bf16[8,384,720]{2,1,0:T(8,128)(2,1)} %bitcast.17, bf16[1440,2880]{1,0:T(8,128)(2,1)} %bitcast.15, bf16[720,2880]{1,0:T(8,128)(2,1)} %bitcast.18, bf16[256,128]{1,0:T(8,128)(2,1)} %bitcast.20, s32[16,16]{1,0:T(8,128)} %bitcast.21), custom_call_target="tpu_custom_call" | custom-call | tf_op jit(solution)/shard_map/run_experts/pallas_call | solution.py:615
  106.1 44.2 %give_back.1 = bf16[64,24,720]{2,1,0:T(8,128)(2,1)} custom-call(bf16[2,64,24,720]{3,2,1,0:T(8,128)(2,1)} %bitcast.16), custom_call_target="tpu_custom_call" | custom-call | tf_op jit(solution)/shard_map/give_back/pallas_call | solution.py:703
  150.3 3.4 %combine.1 = bf16[32,2880]{1,0:T(8,128)(2,1)} custom-call(bf16[1536,720]{1,0:T(8,128)(2,1)} %bitcast.14, f32[32,2880]{1,0:T(8,128)} %get-tuple-element.10.resid_ref, s32[4,32]{1,0:T(4,128)} %bitcast.23, f32[4,32]{1,0:T(4,128)} %bitcast.24, s32[4]{0:T(128)} %len_ref.3, s32[1,1536]{1,0:T(1,128)} %constant.2.clone.shift_ref), custom_call_target="tpu_custom_call" | custom-call | tf_op jit(solution)/shard_map/combine/pallas_call | solution.py:763
